TPU v7x, 256 devices: a whole 4x4x8 slice. The times are simulated.
256 devices in a mesh: row: 8 (over z), col: 32 (over y, x, core).
Axes of the slice: x: 4, y: 4, z: 8, core: 2. Of those that a mesh axis runs over, the one named last changes fastest.
Arguments:
- src_pos: float32 [3, 131072], P(None, 'row'), may hold values from 0 to 10
- tgt_pos: float32 [3, 8192], P(None, 'col'), may hold values from 0 to 20
- src_weight: float32 [131072], P('row'), may hold values from 0.1 to 3
- tgt_weight: float32 [8192], P('col'), may hold values from 0.1 to 3
- src_order: int32 [131072], P('row'), may hold values from 0 to 131071, as said below
- tgt_order: int32 [8192], P('col'), may hold values from 0 to 8191, as said below
- tile_mask: int32 [512, 32], P('row', 'col'), may hold values from 0 to 1, as said below
Outputs:
- src_potential: float32 [131072], P('row')
- tgt_potential: float32 [8192], P('col')
- displacement: float32 [3, 131072], P(None, 'row')
Inputs may be any that keep to these rules, and one draw needn't show every extreme that they name: `src_order`: each aligned block of 16384 entries is a permutation of that block's own indices. `tgt_order`: each aligned block of 256 entries is a permutation of that block's own indices. `tile_mask`: every row and every column of the mask holds at least one kept pair.
All inputs are finite; a program needn't handle non-finite values.
Results may differ from a plain program's by a relative error of at most 0.0003.
Values sent between devices are 32-bit elements; how exact they have to be, the bound alone decides.
No kernel may reach another device: no remote copies, remote signals or barrier semaphores. Data moves between devices by JAX's collectives and lax.ppermute only.
A program may use at most 64 MiB of HBM per device.

v0:
```python
import jax
import jax.numpy as jnp
from jax import lax
from jax.sharding import Mesh
from jax.sharding import PartitionSpec as P

TILE = 256
SWEEPS = 2
COL = ("col_0", "col_1", "col_2")
ROW_COL = ("row", "col_0", "col_1", "col_2")


epsilon = 0.4
lowest = -1e30
block_limit = 1 << 20


def joined_along(pieces, dim):
    pieces = jnp.moveaxis(pieces, 0, dim)
    shape = pieces.shape
    return pieces.reshape(*shape[:dim], shape[dim] * shape[dim + 1], *shape[dim + 2 :])


def gather_packed(arrays, axis, dims):
    line = jnp.concatenate([a.reshape(-1) for a in arrays])
    lines, at, outs = (lax.all_gather(line, axis), 0, [])
    for a, dim in zip(arrays, dims):
        pieces = lines[:, at : at + a.size].reshape(-1, *a.shape)
        outs.append(joined_along(pieces, dim))
        at += a.size
    return tuple(outs)


def collected_together(array, axis):
    leaves = jax.tree.leaves(array)
    order = sorted(range(len(leaves)), key=lambda k: -leaves[k].size)
    width = (1, *leaves[order[0]].shape)[-1]
    lines = [
        jnp.pad(leaves[k].reshape(-1), (0, -leaves[k].size % width)).reshape(-1, width)
        for k in order
    ]
    both, at, found = (lax.all_gather(jnp.concatenate(lines), axis), 0, {})
    for k, line in zip(order, lines):
        share = both[:, at : at + len(line)].reshape(len(both), -1)
        found[k] = share[:, : leaves[k].size].reshape(-1, *leaves[k].shape)
        at += len(line)
    numbers = iter(range(len(leaves)))
    return jax.tree.map(lambda _: found[next(numbers)], array)


def merged_by_axis(array, axes, combine):
    for axis in axes:
        pieces = collected_together(array, axis)
        array = jax.tree.map(lambda part: part[0], pieces)
        for k in range(1, lax.axis_size(axis)):
            array = combine(array, jax.tree.map(lambda part: part[k], pieces))
    return array


def tile_pass(sources, targets, src_terms, tgt_terms, keep_mask, with_shift):
    rows_here = sources.shape[1]
    cols_here = targets.shape[1]
    src_tiles = rows_here // TILE
    tgt_tiles = cols_here // TILE
    block_tiles = max(1, min(src_tiles, block_limit // (TILE * cols_here)))
    while src_tiles % block_tiles != 0:
        block_tiles = block_tiles - 1
    block_rows = block_tiles * TILE
    blocks = src_tiles // block_tiles
    src_split = sources.reshape(3, blocks, block_rows).transpose(1, 0, 2)
    term_split = src_terms.reshape(blocks, block_rows)
    mask_split = keep_mask.reshape(blocks, block_tiles, tgt_tiles)

    def visit(carried, slices):
        col_top, col_sum = carried
        src_block, term_block, mask_block = slices
        distance = 0.5 * sum(
            (
                (src_block[coordinate][:, None] - targets[coordinate][None, :]) ** 2
                for coordinate in range(3)
            )
        )
        scaled = distance / epsilon
        alive = jnp.broadcast_to(
            (mask_block > 0)[:, None, :, None], (block_tiles, TILE, tgt_tiles, TILE)
        ).reshape(block_rows, cols_here)
        toward = tgt_terms[None, :] - scaled
        backward = term_block[:, None] - scaled
        row_top = jnp.max(jnp.where(alive, toward, lowest), axis=1)
        row_exp = jnp.where(alive, jnp.exp(toward - row_top[:, None]), 0.0)
        row_sum = jnp.sum(row_exp, axis=1)
        if with_shift:
            pulled = jnp.dot(row_exp, targets.T, precision=lax.Precision.HIGHEST).T
        else:
            pulled = jnp.zeros((3, block_rows), jnp.float32)
        col_peak = jnp.max(jnp.where(alive, backward, lowest), axis=0)
        renewed = jnp.maximum(col_top, col_peak)
        col_sum = col_sum * jnp.exp(col_top - renewed) + jnp.sum(
            jnp.where(alive, jnp.exp(backward - renewed[None, :]), 0.0), axis=0
        )
        return ((renewed, col_sum), (row_top, row_sum, pulled))

    starting = (jnp.full((cols_here,), lowest, jnp.float32), jnp.zeros((cols_here,), jnp.float32))
    (col_top, col_sum), (row_top, row_sum, pulled) = lax.scan(
        visit, starting, (src_split, term_split, mask_split)
    )
    return (
        row_top.reshape(-1),
        row_sum.reshape(-1),
        pulled.transpose(1, 0, 2).reshape(3, -1),
        col_top,
        col_sum,
    )


def merge_rule(scaled_count):

    def combine(left_part, right_part):
        peak_value = jnp.maximum(left_part[0], right_part[0])
        left_scale = jnp.exp(left_part[0] - peak_value)
        right_scale = jnp.exp(right_part[0] - peak_value)
        merged = [peak_value]
        member = 1
        merged.append(left_part[member] * left_scale + right_part[member] * right_scale)
        for member in range(1 + scaled_count, len(left_part)):
            merged.append(left_part[member] + right_part[member])
        return tuple(merged)

    return combine


def potential(peak_value, total_sum, mass_total):
    return -epsilon * (peak_value + jnp.log(total_sum) - jnp.log(mass_total))


def local(src_pos, tgt_pos, src_weight, tgt_weight, src_order, tgt_order, tile_mask):
    rows_here = src_pos.shape[1]
    cols_here = tgt_pos.shape[1]
    row_at = lax.axis_index("row")
    col_at = lax.axis_index(COL)
    targets = jnp.take(tgt_pos, tgt_order - col_at * cols_here, axis=1)
    tgt_mass = jnp.take(tgt_weight, tgt_order - col_at * cols_here)
    passes = SWEEPS + 2
    src_total = lax.psum(jnp.sum(src_weight), "row")
    col_count = lax.axis_size(COL)
    share_rows = rows_here // col_count
    offset = col_at * share_rows
    part_order = lax.dynamic_slice_in_dim(src_order, offset, share_rows, 0) - row_at * rows_here
    part_src = jnp.take(src_pos, part_order, axis=1)
    part_mass = jnp.take(src_weight, part_order)
    whole_tgt, whole_mass, whole_mask = gather_packed(
        (targets, tgt_mass, tile_mask.astype(jnp.float32)), COL, (1, 0, 1)
    )
    tile_share = share_rows // TILE
    part_mask = (
        lax.dynamic_slice_in_dim(whole_mask, col_at * tile_share, tile_share, 0) > 0.5
    ).astype(jnp.int32)
    tgt_total = jnp.sum(whole_mass)
    log_part = jnp.log(part_mass)
    log_whole = jnp.log(whole_mass)
    src_field = jnp.zeros((share_rows,), jnp.float32)
    tgt_field = jnp.zeros((whole_mass.shape[0],), jnp.float32)
    for sweep_at in range(passes):
        closing = sweep_at == passes - 1
        partial_value = tile_pass(
            part_src,
            whole_tgt,
            log_part + src_field / epsilon,
            log_whole + tgt_field / epsilon,
            part_mask,
            closing,
        )
        col_part = (partial_value[3], partial_value[4])
        col_done = merged_by_axis(col_part, ROW_COL, merge_rule(1))
        src_new = potential(partial_value[0], partial_value[1], tgt_total)
        tgt_new = potential(col_done[0], col_done[1], src_total)
        if sweep_at == 0 or closing:
            src_field, tgt_field = (src_new, tgt_new)
        else:
            src_field = 0.5 * (src_field + src_new)
            tgt_field = 0.5 * (tgt_field + tgt_new)
        if closing:
            part_shift = part_src - partial_value[2] / partial_value[1][None, :]
    src_potential, displacement = gather_packed((src_field, part_shift), COL, (0, 1))
    tgt_potential = lax.dynamic_slice_in_dim(tgt_field, col_at * cols_here, cols_here, 0)
    return (src_potential, tgt_potential, displacement)


def solution(mesh):
    split = Mesh(
        mesh.devices.reshape(mesh.shape["row"], 4, 4, 2), ("row", "col_0", "col_1", "col_2")
    )
    in_specs = (P(None, "row"), P(None, COL), P("row"), P(COL), P("row"), P(COL), P("row", COL))
    out_specs = (P("row"), P(COL), P(None, "row"))
    return jax.shard_map(local, mesh=split, in_specs=in_specs, out_specs=out_specs, check_vma=False)
```

profile of v0, /device:TPU:1, one launch (start us, length us, event | category | flops | bytes accessed | tf_op | source)
XLA Modules:
  0.0 517.0 jit_solution(8127866451320708528)
XLA Ops:
  7.2 0.7 convert_bitcast_fusion
  7.9 0.7 compare_select_fusion.1
  8.6 1.9 gather_fusion.1
  10.5 0.7 broadcast_select_fusion
  11.2 0.8 copy.62
  12.1 0.7 gather_fusion
  13.0 1.3 dynamic-slice.6
  15.1 0.7 copy-done.4
  15.7 5.7 %copy.65 = f32[3,16384]{0,1:T(8,128)} copy(f32[3,16384]{1,0:T(4,128)} %param.15) | data formatting | bytes 393216 | tf_op args[0]
  21.4 0.8 compare_and_fusion
  22.2 4.4 gather_fusion.3
  26.8 3.1 gather_fusion.2
  30.1 0.6 reduce_sum.111
  30.7 18.0 %psum.7 = f32[]{:T(128)} all-reduce(f32[]{:T(128)} %reduce_sum.111), channel_id=1, replica_groups=mesh['row'=8,'col_0'=4,'col_1'=4,'col_2'=2] {'row'}, use_global_device_ids=true, to_apply=%region_8.9 | all-reduce | flops 1 | bytes 8 | tf_op jit(solution)/shard_map/psum | solution.py:144
  49.5 79.4 %all-reduce.3.cloned.1.call-done = f32[34816]{0:T(1024)} async-done(((f32[34816]{0:T(1024)}), f32[34816]{0:T(1024)}) %all-reduce.3.cloned.1.call-update) | async-done | bytes 139280
  128.9 1.0 reshape.4658
  129.9 0.6 log_bitcast_fusion
  132.1 28.3 %while.82 = (s32[]{:T(128)}, f32[8192]{0:T(1024)S(1)}, f32[8192]{0:T(1024)S(1)}, f32[2,256]{1,0:T(2,128)S(1)}, f32[2,256]{1,0:T(2,128)S(1)}, /*index=5*/s32[2,1,...) while((s32[]{:T(128)}, f32[8192]{0:T(1024)S(1)}, ...), condition=%wide.wide.region_5.6_spmd.clone, body=%wide.wide.region_0.5_spmd.clone.sunk | while | flops 67149344 | bytes 1301940 | solution.py:104
  132.5 5.9 %select_reduce_fusion.32 = (f32[256]{0:T(256)S(1)}, f32[32,256]{1,0:T(8,128)S(1)}) fusion(f32[32,256]{1,0:T(8,128)S(1)} %get-tuple-element.1712, f32[32,256]{1,0:T(8,128)S(1)} %sub.3319, f32[256]{0:T(256)S(1)} %bitcast.1565, f32[32,256]{1,0:T(8,128)S(1)} %sub.3320, f32[256]{0:T(256)S(1)} %bitcast.1563, f32[32,256]{1,0:T(8,128)S(1)} %sub.3321, ...), kind=kLoop, calls=%fused_computation.5.clone.clone.1 | loop fusion | flops 31448832 | bytes 168992 | tf_op jit(solution)/shard_map/while/body/eval_jaxpr/reduce_max | solution.py:89
  138.5 7.6 %select_reduce_fusion.33 = (f32[256]{0:T(256)S(1)}, f32[32,256]{1,0:T(8,128)S(1)}) fusion(f32[256]{0:T(256)S(1)} %get-tuple-element.1602, f32[32,256]{1,0:T(8,128)S(1)} %get-tuple-element.1712, f32[32,256]{1,0:T(8,128)S(1)} %sub.3319, f32[256]{0:T(256)S(1)} %bitcast.1566, f32[32,256]{1,0:T(8,128)S(1)} %sub.3320, f32[256]{0:T(256)S(1)} %bitcast.1564, ...), kind=kLoop, calls=%fused_computation.4.clone.clone.1 | loop fusion | flops 35643136 | bytes 202784 | tf_op jit(solution)/shard_map/while/body/eval_jaxpr/reduce_sum | solution.py:91
  146.6 5.9 %select_reduce_fusion.32 = (f32[256]{0:T(256)S(1)}, f32[32,256]{1,0:T(8,128)S(1)}) fusion(f32[32,256]{1,0:T(8,128)S(1)} %get-tuple-element.1712, f32[32,256]{1,0:T(8,128)S(1)} %sub.3319, f32[256]{0:T(256)S(1)} %bitcast.1565, f32[32,256]{1,0:T(8,128)S(1)} %sub.3320, f32[256]{0:T(256)S(1)} %bitcast.1563, f32[32,256]{1,0:T(8,128)S(1)} %sub.3321, ...), kind=kLoop, calls=%fused_computation.5.clone.clone.1 | loop fusion | flops 31448832 | bytes 168992 | tf_op jit(solution)/shard_map/while/body/eval_jaxpr/reduce_max | solution.py:89
  152.6 7.6 %select_reduce_fusion.33 = (f32[256]{0:T(256)S(1)}, f32[32,256]{1,0:T(8,128)S(1)}) fusion(f32[256]{0:T(256)S(1)} %get-tuple-element.1602, f32[32,256]{1,0:T(8,128)S(1)} %get-tuple-element.1712, f32[32,256]{1,0:T(8,128)S(1)} %sub.3319, f32[256]{0:T(256)S(1)} %bitcast.1566, f32[32,256]{1,0:T(8,128)S(1)} %sub.3320, f32[256]{0:T(256)S(1)} %bitcast.1564, ...), kind=kLoop, calls=%fused_computation.4.clone.clone.1 | loop fusion | flops 35643136 | bytes 202784 | tf_op jit(solution)/shard_map/while/body/eval_jaxpr/reduce_sum | solution.py:91
  160.5 21.4 %all-gather.18 = f32[8,2,8192]{2,1,0:T(2,128)S(1)} all-gather(f32[1,2,8192]{2,1,0:T(2,128)S(1)} %maximum_bitcast_fusion), channel_id=3, replica_groups=mesh['row'=8,'col_0'=4,'col_1'=4,'col_2'=2] {'row'}, dimensions={0}, use_global_device_ids=true | all-gather | bytes 589824 | tf_op jit(solution)/shard_map/all_gather | solution.py:42
  181.9 0.7 fusion.181
  182.7 9.4 %all-gather.19 = f32[4,2,8192]{2,1,0:T(2,128)S(1)} all-gather(f32[1,2,8192]{2,1,0:T(2,128)S(1)} %maximum_bitcast_fusion.1), channel_id=4, replica_groups=mesh['row'=8,'col_0'=4,'col_1'=4,'col_2'=2] {'col_0'}, dimensions={0}, use_global_device_ids=true | all-gather | bytes 327680 | tf_op jit(solution)/shard_map/all_gather | solution.py:42
  192.5 9.7 %all-gather.20 = f32[4,2,8192]{2,1,0:T(2,128)S(1)} all-gather(f32[1,2,8192]{2,1,0:T(2,128)S(1)} %maximum_bitcast_fusion.2), channel_id=5, replica_groups=mesh['row'=8,'col_0'=4,'col_1'=4,'col_2'=2] {'col_1'}, dimensions={0}, use_global_device_ids=true | all-gather | bytes 327680 | tf_op jit(solution)/shard_map/all_gather | solution.py:42
  202.6 12.2 %all-gather.21 = f32[2,2,8192]{2,1,0:T(2,128)S(1)} all-gather(f32[1,2,8192]{2,1,0:T(2,128)S(1)} %maximum_bitcast_fusion.3), channel_id=6, replica_groups=mesh['row'=8,'col_0'=4,'col_1'=4,'col_2'=2] {'col_2'}, dimensions={0}, use_global_device_ids=true | all-gather | bytes 196608 | tf_op jit(solution)/shard_map/all_gather | solution.py:42
  214.9 0.8 multiply_add_fusion.2
  216.3 28.3 %while.83 = (s32[]{:T(128)}, f32[8192]{0:T(1024)S(1)}, f32[8192]{0:T(1024)S(1)}, f32[2,256]{1,0:T(2,128)S(1)}, f32[2,256]{1,0:T(2,128)S(1)}, /*index=5*/s32[2,1,...) while((s32[]{:T(128)}, f32[8192]{0:T(1024)S(1)}, ...), condition=%wide.wide.region_14.15_spmd.clone, body=%wide.wide.region_9.14_spmd.clone.sunk | while | flops 67149344 | bytes 1301940 | solution.py:104
  216.7 5.9 %select_reduce_fusion.34 = (f32[256]{0:T(256)S(1)}, f32[32,256]{1,0:T(8,128)S(1)}) fusion(f32[32,256]{1,0:T(8,128)S(1)} %get-tuple-element.1757, f32[32,256]{1,0:T(8,128)S(1)} %sub.3348, f32[256]{0:T(256)S(1)} %bitcast.1571, f32[32,256]{1,0:T(8,128)S(1)} %sub.3349, f32[256]{0:T(256)S(1)} %bitcast.1569, f32[32,256]{1,0:T(8,128)S(1)} %sub.3350, ...), kind=kLoop, calls=%fused_computation.24.clone.clone.1 | loop fusion | flops 31448832 | bytes 168992 | tf_op jit(solution)/shard_map/while/body/eval_jaxpr/reduce_max | solution.py:89
  222.7 7.6 %select_reduce_fusion.35 = (f32[256]{0:T(256)S(1)}, f32[32,256]{1,0:T(8,128)S(1)}) fusion(f32[256]{0:T(256)S(1)} %get-tuple-element.1623, f32[32,256]{1,0:T(8,128)S(1)} %get-tuple-element.1757, f32[32,256]{1,0:T(8,128)S(1)} %sub.3348, f32[256]{0:T(256)S(1)} %bitcast.1572, f32[32,256]{1,0:T(8,128)S(1)} %sub.3349, f32[256]{0:T(256)S(1)} %bitcast.1570, ...), kind=kLoop, calls=%fused_computation.23.clone.clone.1 | loop fusion | flops 35643136 | bytes 202784 | tf_op jit(solution)/shard_map/while/body/eval_jaxpr/reduce_sum | solution.py:91
  230.8 5.9 %select_reduce_fusion.34 = (f32[256]{0:T(256)S(1)}, f32[32,256]{1,0:T(8,128)S(1)}) fusion(f32[32,256]{1,0:T(8,128)S(1)} %get-tuple-element.1757, f32[32,256]{1,0:T(8,128)S(1)} %sub.3348, f32[256]{0:T(256)S(1)} %bitcast.1571, f32[32,256]{1,0:T(8,128)S(1)} %sub.3349, f32[256]{0:T(256)S(1)} %bitcast.1569, f32[32,256]{1,0:T(8,128)S(1)} %sub.3350, ...), kind=kLoop, calls=%fused_computation.24.clone.clone.1 | loop fusion | flops 31448832 | bytes 168992 | tf_op jit(solution)/shard_map/while/body/eval_jaxpr/reduce_max | solution.py:89
  236.8 7.6 %select_reduce_fusion.35 = (f32[256]{0:T(256)S(1)}, f32[32,256]{1,0:T(8,128)S(1)}) fusion(f32[256]{0:T(256)S(1)} %get-tuple-element.1623, f32[32,256]{1,0:T(8,128)S(1)} %get-tuple-element.1757, f32[32,256]{1,0:T(8,128)S(1)} %sub.3348, f32[256]{0:T(256)S(1)} %bitcast.1572, f32[32,256]{1,0:T(8,128)S(1)} %sub.3349, f32[256]{0:T(256)S(1)} %bitcast.1570, ...), kind=kLoop, calls=%fused_computation.23.clone.clone.1 | loop fusion | flops 35643136 | bytes 202784 | tf_op jit(solution)/shard_map/while/body/eval_jaxpr/reduce_sum | solution.py:91
  244.7 19.4 %all-gather.22 = f32[8,2,8192]{2,1,0:T(2,128)S(1)} all-gather(f32[1,2,8192]{2,1,0:T(2,128)S(1)} %maximum_bitcast_fusion.4), channel_id=7, replica_groups=mesh['row'=8,'col_0'=4,'col_1'=4,'col_2'=2] {'row'}, dimensions={0}, use_global_device_ids=true | all-gather | bytes 589824 | tf_op jit(solution)/shard_map/all_gather | solution.py:42
  264.1 0.7 fusion.142
  264.9 9.7 %all-gather.23 = f32[4,2,8192]{2,1,0:T(2,128)S(1)} all-gather(f32[1,2,8192]{2,1,0:T(2,128)S(1)} %maximum_bitcast_fusion.5), channel_id=8, replica_groups=mesh['row'=8,'col_0'=4,'col_1'=4,'col_2'=2] {'col_0'}, dimensions={0}, use_global_device_ids=true | all-gather | bytes 327680 | tf_op jit(solution)/shard_map/all_gather | solution.py:42
  275.0 9.7 %all-gather.24 = f32[4,2,8192]{2,1,0:T(2,128)S(1)} all-gather(f32[1,2,8192]{2,1,0:T(2,128)S(1)} %maximum_bitcast_fusion.6), channel_id=9, replica_groups=mesh['row'=8,'col_0'=4,'col_1'=4,'col_2'=2] {'col_1'}, dimensions={0}, use_global_device_ids=true | all-gather | bytes 327680 | tf_op jit(solution)/shard_map/all_gather | solution.py:42
  285.1 13.5 %all-gather.25 = f32[2,2,8192]{2,1,0:T(2,128)S(1)} all-gather(f32[1,2,8192]{2,1,0:T(2,128)S(1)} %maximum_bitcast_fusion.7), channel_id=10, replica_groups=mesh['row'=8,'col_0'=4,'col_1'=4,'col_2'=2] {'col_2'}, dimensions={0}, use_global_device_ids=true | all-gather | bytes 196608 | tf_op jit(solution)/shard_map/all_gather | solution.py:42
  299.3 28.3 %while.84 = (s32[]{:T(128)}, f32[8192]{0:T(1024)S(1)}, f32[8192]{0:T(1024)S(1)}, f32[2,256]{1,0:T(2,128)S(1)}, f32[2,256]{1,0:T(2,128)S(1)}, /*index=5*/s32[2,1,...) while((s32[]{:T(128)}, f32[8192]{0:T(1024)S(1)}, ...), condition=%wide.wide.region_20.21_spmd.clone, body=%wide.wide.region_15.20_spmd.clone.sunk | while | flops 67149344 | bytes 1301940 | solution.py:104
  299.7 5.9 %select_reduce_fusion.36 = (f32[256]{0:T(256)S(1)}, f32[32,256]{1,0:T(8,128)S(1)}) fusion(f32[32,256]{1,0:T(8,128)S(1)} %get-tuple-element.1802, f32[32,256]{1,0:T(8,128)S(1)} %sub.3377, f32[256]{0:T(256)S(1)} %bitcast.1577, f32[32,256]{1,0:T(8,128)S(1)} %sub.3378, f32[256]{0:T(256)S(1)} %bitcast.1575, f32[32,256]{1,0:T(8,128)S(1)} %sub.3379, ...), kind=kLoop, calls=%fused_computation.43.clone.clone.1 | loop fusion | flops 31448832 | bytes 168992 | tf_op jit(solution)/shard_map/while/body/eval_jaxpr/reduce_max | solution.py:89
  305.7 7.6 %select_reduce_fusion.37 = (f32[256]{0:T(256)S(1)}, f32[32,256]{1,0:T(8,128)S(1)}) fusion(f32[256]{0:T(256)S(1)} %get-tuple-element.1644, f32[32,256]{1,0:T(8,128)S(1)} %get-tuple-element.1802, f32[32,256]{1,0:T(8,128)S(1)} %sub.3377, f32[256]{0:T(256)S(1)} %bitcast.1578, f32[32,256]{1,0:T(8,128)S(1)} %sub.3378, f32[256]{0:T(256)S(1)} %bitcast.1576, ...), kind=kLoop, calls=%fused_computation.42.clone.clone.1 | loop fusion | flops 35643136 | bytes 202784 | tf_op jit(solution)/shard_map/while/body/eval_jaxpr/reduce_sum | solution.py:91
  313.9 5.9 %select_reduce_fusion.36 = (f32[256]{0:T(256)S(1)}, f32[32,256]{1,0:T(8,128)S(1)}) fusion(f32[32,256]{1,0:T(8,128)S(1)} %get-tuple-element.1802, f32[32,256]{1,0:T(8,128)S(1)} %sub.3377, f32[256]{0:T(256)S(1)} %bitcast.1577, f32[32,256]{1,0:T(8,128)S(1)} %sub.3378, f32[256]{0:T(256)S(1)} %bitcast.1575, f32[32,256]{1,0:T(8,128)S(1)} %sub.3379, ...), kind=kLoop, calls=%fused_computation.43.clone.clone.1 | loop fusion | flops 31448832 | bytes 168992 | tf_op jit(solution)/shard_map/while/body/eval_jaxpr/reduce_max | solution.py:89
  319.9 7.6 %select_reduce_fusion.37 = (f32[256]{0:T(256)S(1)}, f32[32,256]{1,0:T(8,128)S(1)}) fusion(f32[256]{0:T(256)S(1)} %get-tuple-element.1644, f32[32,256]{1,0:T(8,128)S(1)} %get-tuple-element.1802, f32[32,256]{1,0:T(8,128)S(1)} %sub.3377, f32[256]{0:T(256)S(1)} %bitcast.1578, f32[32,256]{1,0:T(8,128)S(1)} %sub.3378, f32[256]{0:T(256)S(1)} %bitcast.1576, ...), kind=kLoop, calls=%fused_computation.42.clone.clone.1 | loop fusion | flops 35643136 | bytes 202784 | tf_op jit(solution)/shard_map/while/body/eval_jaxpr/reduce_sum | solution.py:91
  327.7 19.8 %all-gather.26 = f32[8,2,8192]{2,1,0:T(2,128)S(1)} all-gather(f32[1,2,8192]{2,1,0:T(2,128)S(1)} %maximum_bitcast_fusion.8), channel_id=11, replica_groups=mesh['row'=8,'col_0'=4,'col_1'=4,'col_2'=2] {'row'}, dimensions={0}, use_global_device_ids=true | all-gather | bytes 589824 | tf_op jit(solution)/shard_map/all_gather | solution.py:42
  347.6 0.7 fusion.103
  348.4 9.6 %all-gather.27 = f32[4,2,8192]{2,1,0:T(2,128)S(1)} all-gather(f32[1,2,8192]{2,1,0:T(2,128)S(1)} %maximum_bitcast_fusion.9), channel_id=12, replica_groups=mesh['row'=8,'col_0'=4,'col_1'=4,'col_2'=2] {'col_0'}, dimensions={0}, use_global_device_ids=true | all-gather | bytes 327680 | tf_op jit(solution)/shard_map/all_gather | solution.py:42
  358.4 10.0 %all-gather.28 = f32[4,2,8192]{2,1,0:T(2,128)S(1)} all-gather(f32[1,2,8192]{2,1,0:T(2,128)S(1)} %maximum_bitcast_fusion.10), channel_id=13, replica_groups=mesh['row'=8,'col_0'=4,'col_1'=4,'col_2'=2] {'col_1'}, dimensions={0}, use_global_device_ids=true | all-gather | bytes 327680 | tf_op jit(solution)/shard_map/all_gather | solution.py:42
  368.7 12.3 %all-gather.29 = f32[2,2,8192]{2,1,0:T(2,128)S(1)} all-gather(f32[1,2,8192]{2,1,0:T(2,128)S(1)} %maximum_bitcast_fusion.11), channel_id=14, replica_groups=mesh['row'=8,'col_0'=4,'col_1'=4,'col_2'=2] {'col_2'}, dimensions={0}, use_global_device_ids=true | all-gather | bytes 196608 | tf_op jit(solution)/shard_map/all_gather | solution.py:42
  381.2 48.8 %while.85 = (s32[]{:T(128)}, f32[8192]{0:T(1024)S(1)}, f32[8192]{0:T(1024)S(1)}, f32[2,256]{1,0:T(2,128)S(1)}, f32[2,256]{1,0:T(2,128)S(1)}, /*index=5*/f32[2,3,...) while((s32[]{:T(128)}, f32[8192]{0:T(1024)S(1)}, ...), condition=%wide.wide.region_26.27_spmd.clone, body=%wide.wide.region_21.26_spmd.clone.sunk | while | flops 167812640 | bytes 1703392 | solution.py:104
  381.9 5.9 %select_reduce_fusion.38 = (f32[256]{0:T(256)S(1)}, f32[32,256]{1,0:T(8,128)S(1)}) fusion(f32[32,256]{1,0:T(8,128)S(1)} %get-tuple-element.1850, f32[32,256]{1,0:T(8,128)S(1)} %sub.3419, f32[256]{0:T(256)S(1)} %bitcast.1554, f32[32,256]{1,0:T(8,128)S(1)} %sub.3420, f32[256]{0:T(256)S(1)} %bitcast.1551, f32[32,256]{1,0:T(8,128)S(1)} %sub.3421, ...), kind=kLoop, calls=%fused_computation.76.clone.clone.1 | loop fusion | flops 31448832 | bytes 168992 | tf_op jit(solution)/shard_map/while/body/eval_jaxpr/reduce_max | solution.py:89
  387.9 7.7 %select_reduce_fusion.39 = (f32[256]{0:T(256)S(1)}, f32[32,256]{1,0:T(8,128)S(1)}) fusion(f32[256]{0:T(256)S(1)} %get-tuple-element.1666, f32[32,256]{1,0:T(8,128)S(1)} %get-tuple-element.1850, f32[32,256]{1,0:T(8,128)S(1)} %sub.3419, f32[256]{0:T(256)S(1)} %bitcast.1555, f32[32,256]{1,0:T(8,128)S(1)} %sub.3420, f32[256]{0:T(256)S(1)} %bitcast.1552, ...), kind=kLoop, calls=%fused_computation.75.clone.clone.1 | loop fusion | flops 35643136 | bytes 202784 | tf_op jit(solution)/shard_map/while/body/eval_jaxpr/reduce_sum | solution.py:91
  395.8 10.0 %fusion.304 = f32[2,3,256]{2,1,0:T(4,128)S(1)} fusion(f32[2,3,256]{2,1,0:T(4,128)S(1)} %get-tuple-element.1828, s32[]{:T(128)S(6)} %copy.175, f32[3,8192]{1,0:T(4,128)S(1)} %get-tuple-element.1848, f32[256]{0:T(256)S(1)} %get-tuple-element.1666, f32[8192]{0:T(1024)S(1)} %bitcast.1525, f32[256]{0:T(256)S(1)} %bitcast.1556, ...), kind=kOutput, calls=%fused_computation.94.clone.clone.1 | convolution fusion | flops 100663296 | bytes 278532 | tf_op jit(solution)/shard_map/while/body/eval_jaxpr/dot_general | solution.py:93
  406.2 5.9 %select_reduce_fusion.38 = (f32[256]{0:T(256)S(1)}, f32[32,256]{1,0:T(8,128)S(1)}) fusion(f32[32,256]{1,0:T(8,128)S(1)} %get-tuple-element.1850, f32[32,256]{1,0:T(8,128)S(1)} %sub.3419, f32[256]{0:T(256)S(1)} %bitcast.1554, f32[32,256]{1,0:T(8,128)S(1)} %sub.3420, f32[256]{0:T(256)S(1)} %bitcast.1551, f32[32,256]{1,0:T(8,128)S(1)} %sub.3421, ...), kind=kLoop, calls=%fused_computation.76.clone.clone.1 | loop fusion | flops 31448832 | bytes 168992 | tf_op jit(solution)/shard_map/while/body/eval_jaxpr/reduce_max | solution.py:89
  412.2 7.7 %select_reduce_fusion.39 = (f32[256]{0:T(256)S(1)}, f32[32,256]{1,0:T(8,128)S(1)}) fusion(f32[256]{0:T(256)S(1)} %get-tuple-element.1666, f32[32,256]{1,0:T(8,128)S(1)} %get-tuple-element.1850, f32[32,256]{1,0:T(8,128)S(1)} %sub.3419, f32[256]{0:T(256)S(1)} %bitcast.1555, f32[32,256]{1,0:T(8,128)S(1)} %sub.3420, f32[256]{0:T(256)S(1)} %bitcast.1552, ...), kind=kLoop, calls=%fused_computation.75.clone.clone.1 | loop fusion | flops 35643136 | bytes 202784 | tf_op jit(solution)/shard_map/while/body/eval_jaxpr/reduce_sum | solution.py:91
  420.1 10.0 %fusion.304 = f32[2,3,256]{2,1,0:T(4,128)S(1)} fusion(f32[2,3,256]{2,1,0:T(4,128)S(1)} %get-tuple-element.1828, s32[]{:T(128)S(6)} %copy.175, f32[3,8192]{1,0:T(4,128)S(1)} %get-tuple-element.1848, f32[256]{0:T(256)S(1)} %get-tuple-element.1666, f32[8192]{0:T(1024)S(1)} %bitcast.1525, f32[256]{0:T(256)S(1)} %bitcast.1556, ...), kind=kOutput, calls=%fused_computation.94.clone.clone.1 | convolution fusion | flops 100663296 | bytes 278532 | tf_op jit(solution)/shard_map/while/body/eval_jaxpr/dot_general | solution.py:93
  430.2 24.1 %all-gather.13 = f32[65536]{0:T(1024)S(1)} all-gather(f32[2048]{0:T(1024)S(1)} %pad_maximum_fusion), channel_id=15, replica_groups=mesh['row'=8,'col_0'=4,'col_1'=4,'col_2'=2] {'col_0','col_1','col_2'}, dimensions={0}, use_global_device_ids=true | all-gather | bytes 270336 | tf_op jit(solution)/shard_map/all_gather | solution.py:26
  454.4 0.6 copy.87
  455.1 19.8 %all-gather.30 = f32[8,2,8192]{2,1,0:T(2,128)S(1)} all-gather(f32[1,2,8192]{2,1,0:T(2,128)S(1)} %maximum_bitcast_fusion.12), channel_id=16, replica_groups=mesh['row'=8,'col_0'=4,'col_1'=4,'col_2'=2] {'row'}, dimensions={0}, use_global_device_ids=true | all-gather | bytes 589824 | tf_op jit(solution)/shard_map/all_gather | solution.py:42
  474.9 0.7 fusion.64
  475.7 9.7 %all-gather.31 = f32[4,2,8192]{2,1,0:T(2,128)S(1)} all-gather(f32[1,2,8192]{2,1,0:T(2,128)S(1)} %maximum_bitcast_fusion.13), channel_id=17, replica_groups=mesh['row'=8,'col_0'=4,'col_1'=4,'col_2'=2] {'col_0'}, dimensions={0}, use_global_device_ids=true | all-gather | bytes 327680 | tf_op jit(solution)/shard_map/all_gather | solution.py:42
  485.8 9.7 %all-gather.32 = f32[4,2,8192]{2,1,0:T(2,128)S(1)} all-gather(f32[1,2,8192]{2,1,0:T(2,128)S(1)} %maximum_bitcast_fusion.14), channel_id=18, replica_groups=mesh['row'=8,'col_0'=4,'col_1'=4,'col_2'=2] {'col_1'}, dimensions={0}, use_global_device_ids=true | all-gather | bytes 327680 | tf_op jit(solution)/shard_map/all_gather | solution.py:42
  495.9 12.6 %all-gather.33 = f32[2,2,8192]{2,1,0:T(2,128)S(1)} all-gather(f32[1,2,8192]{2,1,0:T(2,128)S(1)} %maximum_bitcast_fusion.15), channel_id=19, replica_groups=mesh['row'=8,'col_0'=4,'col_1'=4,'col_2'=2] {'col_2'}, dimensions={0}, use_global_device_ids=true | all-gather | bytes 196608 | tf_op jit(solution)/shard_map/all_gather | solution.py:42
  508.6 0.8 reshape.4622
  509.5 0.6 fusion.264
  (229 shorter events, 11.2 us)
Async XLA Ops:
  7.2 1.4 copy-start
  7.2 19.6 %copy-start.1 = (f32[16384]{0:T(1024)S(1)}, f32[16384]{0:T(1024)}, u32[]{:S(2)}) copy-start(f32[16384]{0:T(1024)} %param.17) | copy-start | bytes 196612
  7.2 121.7 %all-reduce.3.cloned.1.call-start = ((), (), s32[]{:S(2)}) async-start(), calls=%async_computation | async-start | bytes 278528
  15.1 0.7 copy-start.4
  131.5 0.6 copy-start.2
  215.7 0.6 copy-start.5
  216.3 82.4 %copy-start.3 = (f32[8192]{0:T(1024)S(1)}, f32[8192]{0:T(1024)}, u32[]{:S(2)}) copy-start(f32[8192]{0:T(1024)} %get-tuple-element.1859) | copy-start | bytes 98308
  298.7 0.6 copy-start.6
Sparse Core Ops, SparseCore 0:
  15.9 112.9 all-reduce.2
where the time goes:
time: 518 us; the launch traced here: 517 us
  blocking collectives  250 us (48%)
  other arithmetic  122 us (24%)
  waiting for transfers between devices  79.4 us (15%)
  local copies, waits for them, and re-layouts  27.7 us (5%)
  matrix products  20 us (4%)
  between operations  16.6 us (3%)
    all_gather x16, blocking collectives, collected_together(): both, at, found = (lax.all_gather(jnp.concatenate(lines), axis), 0, {})  208 us
    unnamed x2, waiting for transfers between devices  79.4 us
    reduce_sum x8, other arithmetic, visit(): row_sum = jnp.sum(row_exp, axis=1)  61.1 us
    reduce_max x8, other arithmetic, visit(): row_top = jnp.max(jnp.where(alive, toward, lowest), axis=1)  47.5 us
    all_gather x1, blocking collectives, gather_packed(): lines, at, outs = (lax.all_gather(line, axis), 0, [])  24.1 us
    dot_general x2, matrix products, visit(): pulled = jnp.dot(row_exp, targets.T, precision=lax.Precision.HIGHEST).T  20 us
    psum x1, blocking collectives, local(): src_total = lax.psum(jnp.sum(src_weight), 'row')  18 us
    unnamed x24, local copies, waits for them, and re-layouts  10.9 us
  transfers between devices with their start and end apart: 1, of which 1 were waited for; matrix products, arithmetic and copies ran while one was open for 3% of the time, Pallas kernels for 0%

commit v1 on v0

v1 whole, which is shorter than its diff:
```python
import jax
import jax.numpy as jnp
from jax import lax
from jax.experimental import pallas as pl
from jax.experimental.pallas import tpu as pltpu
from jax.sharding import Mesh
from jax.sharding import PartitionSpec as P

epsilon = 0.4
LOG2E = 1.4426950408889634
LN2 = 0.6931471805599453
ALPHA = LOG2E / epsilon
HALF = 0.5 * ALPHA
UNIT = epsilon * LN2
CENTRE = 7.5
LOWEST = -(2.0**100)
TILE = 256
LANES = 128

ROW = "row"
SPLIT = ("x",)
MERGE = ("y", "core")
COLS = ("y", "x", "core")

BIAS_S, BIAS_T, MASK0, LOG_S, RAW_S, LOG_T = 3, 4, 5, 9, 10, 13


def f32(shape):
    return jax.ShapeDtypeStruct(shape, jnp.float32)


def call(body, outs, scratch=(), smem=()):
    def run(*args):
        specs = [
            pl.BlockSpec(memory_space=pltpu.SMEM if k in smem else pltpu.VMEM)
            for k in range(len(args))
        ]
        return pl.pallas_call(
            body,
            out_shape=outs,
            in_specs=specs,
            out_specs=jax.tree.map(lambda _: pl.BlockSpec(memory_space=pltpu.VMEM), outs),
            scratch_shapes=list(scratch),
            compiler_params=pltpu.CompilerParams(vmem_limit_bytes=48 << 20),
        )(*args)

    return run


def parts(u):
    hi = u.astype(jnp.bfloat16)
    rest = u - hi.astype(jnp.float32)
    mid = rest.astype(jnp.bfloat16)
    low = (rest - mid.astype(jnp.float32)).astype(jnp.bfloat16)
    return hi, mid, low


def right_side(u, out_ref):
    hi, mid, low = parts(u)
    zero = jnp.zeros_like(hi)
    out_ref[...] = jnp.concatenate([hi, mid, hi, mid, low, hi, zero, zero], axis=0)


def left_side(u, out_ref):
    hi, mid, low = (p.astype(jnp.float32) for p in parts(u))
    zero = jnp.zeros_like(hi)
    stacked = jnp.concatenate([hi, hi, mid, mid, hi, low, zero, zero], axis=0)
    for c in range(u.shape[1] // LANES):
        block = stacked[:, c * LANES : (c + 1) * LANES]
        out_ref[c * LANES : (c + 1) * LANES, :] = block.T.astype(jnp.bfloat16)


def with_row(u, at, row):
    rows = lax.broadcasted_iota(jnp.int32, u.shape, 0)
    return jnp.where(rows == at, row, u)


def row_block(left_ref, right, pull_refs=None):
    x = jnp.dot(left_ref[...], right, preferred_element_type=jnp.float32)
    n = x.shape[1]
    x = x.reshape(x.shape[0] // 8, 8, n)
    top = jnp.max(x, axis=0)
    p = jnp.exp2(x - top[None])
    total = jnp.sum(p, axis=0)
    peak = jnp.max(top, axis=0, keepdims=True)
    weight = jnp.exp2(top - peak)
    sums = jnp.sum(total * weight, axis=0, keepdims=True)
    value = peak + jnp.log2(sums)
    if pull_refs is None:
        return value
    means = []
    for d in range(3):
        wide = jnp.concatenate([pull_refs[d]] * (n // LANES), axis=1)
        moved = jnp.sum(p * wide.reshape(-1, 8, n), axis=0)
        means.append(jnp.sum(moved * weight, axis=0, keepdims=True) / sums)
    return value, means


def row_pass(left_ref, right_ref, emit, width=TILE, pull_refs=None):
    blocks = right_ref.shape[1] // width

    def step(b, carry):
        at = pl.multiple_of(b * width, width)
        emit(at, row_block(left_ref, right_ref[:, pl.ds(at, width)], pull_refs))
        return carry

    lax.fori_loop(0, blocks, step, 0)


def col_pass(left_ref, right_ref, top_ref, sum_ref, width=1024):
    m = left_ref.shape[0]
    n = right_ref.shape[1]
    for t in range(m // TILE):
        rows = slice(t * TILE, (t + 1) * TILE)

        def step(b, carry):
            top_old, sum_old = carry
            at = pl.multiple_of(b * width, width)
            x = jnp.dot(
                left_ref[rows, :],
                right_ref[:, pl.ds(at, width)],
                preferred_element_type=jnp.float32,
            )
            cuts = [x[:, k * LANES : (k + 1) * LANES] for k in range(width // LANES)]
            top = top_old
            for cut in cuts:
                top = jnp.maximum(top, cut)
            total = sum_old * jnp.exp2(top_old - top)
            for cut in cuts:
                total = total + jnp.exp2(cut - top)
            return top, total

        start = (
            jnp.full((TILE, LANES), 2.0 * LOWEST, jnp.float32),
            jnp.zeros((TILE, LANES), jnp.float32),
        )
        top, total = lax.fori_loop(0, n // width, step, start)
        top_ref[rows, :] = top
        sum_ref[rows, :] = total
    found = []
    for c in range(m // LANES):
        top = top_ref[c * LANES : (c + 1) * LANES, :].T
        total = sum_ref[c * LANES : (c + 1) * LANES, :].T
        peak = jnp.max(top, axis=0, keepdims=True)
        sums = jnp.sum(total * jnp.exp2(top - peak), axis=0, keepdims=True)
        found.append(peak + jnp.log2(sums))
    return jnp.concatenate(found, axis=1)


def merged(values):
    peak = jnp.max(values, axis=0, keepdims=True)
    return peak + jnp.log2(jnp.sum(jnp.exp2(values - peak), axis=0, keepdims=True))


def lane_gather(table, lanes):
    return jnp.take_along_axis(table, lanes, axis=1, mode="promise_in_bounds")


def pack_targets(pos_ref, weight_ref, order_ref, mask_ref, out_ref):
    order = jnp.bitwise_and(order_ref[...], TILE - 1)
    high = jnp.right_shift(order, 7)
    low = jnp.bitwise_and(order, LANES - 1)
    high8 = jnp.concatenate([high] * 4, axis=0)
    low8 = jnp.concatenate([low] * 4, axis=0)
    found = jnp.zeros((8, LANES), jnp.float32)
    for r in range(2):
        lanes = slice(r * LANES, (r + 1) * LANES)
        lines = [jnp.broadcast_to(pos_ref[d : d + 1, lanes], (2, LANES)) for d in range(3)]
        lines.append(jnp.broadcast_to(weight_ref[r : r + 1, :], (2, LANES)))
        table = jnp.concatenate(lines, axis=0)
        found = jnp.where(high8 == r, lane_gather(table, low8), found)
    tiles = mask_ref.shape[0]
    at = lax.broadcasted_iota(jnp.int32, (tiles, LANES), 0)
    lane = lax.broadcasted_iota(jnp.int32, (tiles, LANES), 1)
    kept = jnp.broadcast_to(mask_ref[...].astype(jnp.float32), (tiles, LANES))
    line = jnp.sum(jnp.where(at == lane, kept, 0.0), axis=0, keepdims=True)
    both = jnp.concatenate([found, jnp.broadcast_to(line, (8, LANES))], axis=0)
    for k in range(out_ref.shape[0]):
        out_ref[k] = both


def first_rows(
    quarter_ref, got_ref, pos_ref, weight_ref, order_ref, src_ref, tgt_ref, out_ref,
    left_ref, right_ref,
):
    quarter = quarter_ref[0]
    n = src_ref.shape[1]
    lines = n // LANES
    groups = lines // 8
    order = order_ref[pl.ds(pl.multiple_of(quarter * lines, 8), lines), :]
    order = jnp.bitwise_and(order, LANES * LANES - 1)
    high = jnp.right_shift(order, 7)
    low = jnp.bitwise_and(order, LANES - 1)
    highs = [high[8 * g : 8 * g + 8] for g in range(groups)]
    lows = [low[8 * g : 8 * g + 8] for g in range(groups)]

    def look(r, found):
        at = pl.multiple_of(r * LANES, LANES)
        tables = [
            jnp.broadcast_to(pos_ref[d : d + 1, pl.ds(at, LANES)], (8, LANES)) for d in range(3)
        ]
        tables.append(jnp.broadcast_to(weight_ref[pl.ds(r, 1), :], (8, LANES)))
        out = []
        for g in range(groups):
            here = highs[g] == r
            for a in range(4):
                old = found[4 * g + a]
                out.append(jnp.where(here, lane_gather(tables[a], lows[g]), old))
        return tuple(out)

    zero = jnp.zeros((8, LANES), jnp.float32)
    found = lax.fori_loop(0, LANES, look, (zero,) * (4 * groups), unroll=4)

    src_ref[...] = jnp.zeros_like(src_ref)
    for g in range(groups):
        for k in range(8):
            lanes = slice((8 * g + k) * LANES, (8 * g + k + 1) * LANES)
            for d in range(3):
                src_ref[RAW_S + d : RAW_S + d + 1, lanes] = found[4 * g + d][k : k + 1, :] - CENTRE
            src_ref[LOG_S : LOG_S + 1, lanes] = found[4 * g + 3][k : k + 1, :]
    square = jnp.zeros((1, n), jnp.float32)
    for d in range(3):
        raw = src_ref[RAW_S + d : RAW_S + d + 1, :]
        src_ref[d : d + 1, :] = ALPHA * raw
        square = square + raw * raw
    src_ref[BIAS_S : BIAS_S + 1, :] = -HALF * square
    src_ref[BIAS_T : BIAS_T + 1, :] = jnp.ones((1, n), jnp.float32)
    src_ref[LOG_S : LOG_S + 1, :] = jnp.log2(src_ref[LOG_S : LOG_S + 1, :])

    tiles = got_ref.shape[0]
    m = tgt_ref.shape[1]
    tgt_ref[...] = jnp.zeros_like(tgt_ref)
    flags = jnp.concatenate([got_ref[t][8:9, :] for t in range(tiles)] * 2, axis=0)
    src_tiles = n // TILE
    flags = pltpu.roll(flags, (LANES - quarter * src_tiles) % LANES, 1)
    bias = jnp.where(flags > 0.5, 0.0, LOWEST)
    for i in range(src_tiles):
        src_ref[MASK0 : MASK0 + tiles, i * TILE : (i + 1) * TILE] = jnp.broadcast_to(
            bias[:tiles, i : i + 1], (tiles, TILE)
        )
    mass = jnp.zeros((1, LANES), jnp.float32)
    for t in range(tiles):
        for k in range(2):
            lanes = slice(t * TILE + k * LANES, t * TILE + (k + 1) * LANES)
            square = jnp.zeros((1, LANES), jnp.float32)
            for d in range(3):
                raw = got_ref[t][2 * d + k : 2 * d + k + 1, :] - CENTRE
                tgt_ref[d : d + 1, lanes] = raw
                square = square + raw * raw
            tgt_ref[BIAS_T : BIAS_T + 1, lanes] = -HALF * square
            weight = got_ref[t][6 + k : 7 + k, :]
            tgt_ref[LOG_T : LOG_T + 1, lanes] = jnp.log2(weight)
            mass = mass + weight
        tgt_ref[MASK0 + t : MASK0 + t + 1, t * TILE : (t + 1) * TILE] = jnp.ones(
            (1, TILE), jnp.float32
        )
    tgt_ref[BIAS_S : BIAS_S + 1, :] = jnp.ones((1, m), jnp.float32)

    tgt = tgt_ref[...]
    bias_t = tgt_ref[BIAS_T : BIAS_T + 1, :] + tgt_ref[LOG_T : LOG_T + 1, :]
    left_side(with_row(tgt, BIAS_T, bias_t), left_ref)
    right_side(src_ref[...], right_ref)
    copies = out_ref.shape[0]

    def emit(at, value):
        out_ref[:, pl.ds(at, TILE)] = jnp.broadcast_to(value, (copies, TILE))

    row_pass(left_ref, right_ref, emit)
    whole = jnp.sum(mass, axis=1, keepdims=True)
    out_ref[:, n:] = jnp.broadcast_to(whole, (copies, LANES))


def first_cols(got_ref, src_ref, tgt_ref, field_ref, out_ref, left_ref, right_ref, top_ref, sum_ref):
    n = src_ref.shape[1]
    m = tgt_ref.shape[1]
    tgt_total = jnp.log2(jnp.sum(got_ref[:, n:], axis=0, keepdims=True))
    field = -(merged(got_ref[:, :n]) - tgt_total[:, :1])
    field_ref[0:1, :] = field
    field_ref[1:2, :] = jnp.broadcast_to(tgt_total[:, :1], (1, n))
    left_side(tgt_ref[...], left_ref)
    log_mass = src_ref[LOG_S : LOG_S + 1, :]
    bias = src_ref[BIAS_S : BIAS_S + 1, :] + log_mass
    copies = out_ref.shape[0]
    for k, term in enumerate((bias, bias + field)):
        right_side(with_row(src_ref[...], BIAS_S, term), right_ref)
        value = col_pass(left_ref, right_ref, top_ref, sum_ref)
        out_ref[:, k * m : (k + 1) * m] = jnp.broadcast_to(value, (copies, m))
    mass = jnp.sum(jnp.exp2(log_mass), axis=1, keepdims=True)
    out_ref[:, 2 * m :] = jnp.broadcast_to(mass, (copies, LANES))


def middle_rows(got_ref, src_ref, tgt_ref, field_ref, out_ref, left_ref, right_ref):
    n = src_ref.shape[1]
    m = tgt_ref.shape[1]
    src_total = jnp.log2(jnp.sum(got_ref[:, 2 * m :], axis=0, keepdims=True))[:, :1]
    start = -(merged(got_ref[:, :m]) - src_total)
    once = 0.5 * (start - (merged(got_ref[:, m : 2 * m]) - src_total))
    field_ref[0:1, :] = once
    field_ref[1:2, :] = jnp.broadcast_to(src_total, (1, m))
    right_side(src_ref[...], right_ref)
    base = tgt_ref[BIAS_T : BIAS_T + 1, :] + tgt_ref[LOG_T : LOG_T + 1, :]
    copies = out_ref.shape[0]
    for k, term in enumerate((start, once)):
        left_side(with_row(tgt_ref[...], BIAS_T, base + term), left_ref)

        def emit(at, value, k=k):
            out_ref[:, pl.ds(k * n + at, TILE)] = jnp.broadcast_to(value, (copies, TILE))

        row_pass(left_ref, right_ref, emit)


def middle_cols(got_ref, src_ref, tgt_ref, field_ref, out_ref, left_ref, right_ref, top_ref, sum_ref):
    n = src_ref.shape[1]
    m = tgt_ref.shape[1]
    tgt_total = field_ref[1:2, :]
    once = 0.5 * (field_ref[0:1, :] - (merged(got_ref[:, :n]) - tgt_total))
    twice = 0.5 * (once - (merged(got_ref[:, n:]) - tgt_total))
    left_side(tgt_ref[...], left_ref)
    bias = src_ref[BIAS_S : BIAS_S + 1, :] + src_ref[LOG_S : LOG_S + 1, :]
    copies = out_ref.shape[0]
    for k, term in enumerate((once, twice)):
        right_side(with_row(src_ref[...], BIAS_S, bias + term), right_ref)
        value = col_pass(left_ref, right_ref, top_ref, sum_ref)
        out_ref[:, k * m : (k + 1) * m] = jnp.broadcast_to(value, (copies, m))


def last_rows(
    quarter_ref, got_ref, src_ref, tgt_ref, field_ref, scale_ref, out_ref, own_ref,
    left_ref, right_ref, pull_ref, line_ref,
):
    n = src_ref.shape[1]
    m = tgt_ref.shape[1]
    src_total = field_ref[1:2, :]
    twice = 0.5 * (field_ref[0:1, :] - (merged(got_ref[:, :m]) - src_total))
    line_ref[...] = -UNIT * (merged(got_ref[:, m:]) - src_total)
    own_ref[...] = line_ref[:, pl.ds(pl.multiple_of(quarter_ref[0] * TILE, TILE), TILE)]
    right_side(src_ref[...], right_ref)
    base = tgt_ref[BIAS_T : BIAS_T + 1, :] + tgt_ref[LOG_T : LOG_T + 1, :]
    left_side(with_row(tgt_ref[...], BIAS_T, base + twice), left_ref)
    for d in range(3):
        for c in range(m // LANES):
            lanes = slice(c * LANES, (c + 1) * LANES)
            wide = jnp.broadcast_to(tgt_ref[d : d + 1, lanes], (LANES, LANES))
            pull_ref[d, lanes, :] = wide.T
    tgt_total = scale_ref[1:2, 0:1]
    share = n // out_ref.shape[0]
    pulls = [pull_ref[d] for d in range(3)]

    def emit(at, found):
        value, means = found
        piece = at // share
        lane = pl.multiple_of(at - piece * share, TILE)
        out_ref[pl.ds(piece, 1), 0:1, pl.ds(lane, TILE)] = (value - tgt_total)[None]
        for d in range(3):
            raw = src_ref[RAW_S + d : RAW_S + d + 1, pl.ds(at, TILE)]
            out_ref[pl.ds(piece, 1), d + 1 : d + 2, pl.ds(lane, TILE)] = (raw - means[d])[None]

    row_pass(left_ref, right_ref, emit, pull_refs=pulls)


def closing(got_ref, out_ref):
    values = got_ref[:, 0, :]
    peak = jnp.max(values, axis=0, keepdims=True)
    weight = jnp.exp2(values - peak)
    total = jnp.sum(weight, axis=0, keepdims=True)
    lines = [-UNIT * (peak + jnp.log2(total))]
    for d in range(3):
        lines.append(jnp.sum(weight * got_ref[:, d + 1, :], axis=0, keepdims=True) / total)
    both = jnp.concatenate(lines, axis=0)
    for k in range(out_ref.shape[0]):
        out_ref[k] = both


def spread(got_ref, value_ref, shift_ref):
    share = got_ref.shape[2]
    for k in range(got_ref.shape[0]):
        lanes = slice(k * share, (k + 1) * share)
        value_ref[:, lanes] = got_ref[k][0:1, :]
        shift_ref[:, lanes] = got_ref[k][1:4, :]


def exchange(array, axes):
    return lax.all_to_all(array, axes, 0, 0, tiled=True)


def local(src_pos, tgt_pos, src_weight, tgt_weight, src_order, tgt_order, tile_mask):
    rows_here = src_pos.shape[1]
    splits = lax.axis_size(SPLIT)
    merges = lax.axis_size(MERGE)
    heights = lax.axis_size((ROW,) + SPLIT)
    n = rows_here // splits
    m = tgt_pos.shape[1] * splits
    quarter = lax.axis_index(SPLIT).astype(jnp.int32).reshape(1)
    left = pltpu.VMEM((m, LANES), jnp.bfloat16)
    right = pltpu.VMEM((LANES, n), jnp.bfloat16)
    wide = pltpu.VMEM((m, LANES), jnp.float32)

    packed = call(pack_targets, f32((splits, 16, LANES)))(
        tgt_pos,
        tgt_weight.reshape(-1, LANES),
        tgt_order.reshape(-1, LANES),
        tile_mask,
    )
    packed = exchange(packed, SPLIT)
    src, tgt, row0 = call(
        first_rows, (f32((16, n)), f32((16, m)), f32((merges, n + LANES))), (left, right), (0,)
    )(quarter, packed, src_pos, src_weight.reshape(-1, LANES), src_order.reshape(-1, LANES))
    row0 = exchange(row0, MERGE)
    src_field, col01 = call(
        first_cols, (f32((2, n)), f32((heights, 2 * m + LANES))), (left, right, wide, wide)
    )(row0, src, tgt)
    col01 = exchange(col01, (ROW,) + SPLIT)
    tgt_field, row12 = call(middle_rows, (f32((2, m)), f32((merges, 2 * n))), (left, right))(
        col01, src, tgt
    )
    row12 = exchange(row12, MERGE)
    col23 = call(middle_cols, f32((heights, 2 * m)), (left, right, wide, wide))(
        row12, src, tgt, src_field
    )
    col23 = exchange(col23, (ROW,) + SPLIT)
    row3, own = call(
        last_rows,
        (f32((merges, 4, n // merges)), f32((1, TILE))),
        (left, right, pltpu.VMEM((3, m, LANES), jnp.float32), pltpu.VMEM((1, m), jnp.float32)),
        (0,),
    )(quarter, col23, src, tgt, tgt_field, src_field)
    row3 = exchange(row3, MERGE)
    everyone = SPLIT + MERGE
    done = call(closing, f32((lax.axis_size(everyone), 4, n // merges)))(row3)
    done = exchange(done, everyone)
    value, shift = call(spread, (f32((1, rows_here)), f32((3, rows_here))))(done)
    return value.reshape(-1), own.reshape(-1), shift


def solution(mesh):
    split = Mesh(mesh.devices.reshape(mesh.shape["row"], 4, 4, 2), ("row", "y", "x", "core"))
    in_specs = (P(None, ROW), P(None, COLS), P(ROW), P(COLS), P(ROW), P(COLS), P(ROW, COLS))
    out_specs = (P(ROW), P(COLS), P(None, ROW))
    return jax.shard_map(local, mesh=split, in_specs=in_specs, out_specs=out_specs, check_vma=False)
```

time: 518 us -> 169 us (0.33)
  blocking collectives: 250 us -> 81.3 us
  other arithmetic: 122 us -> 0 us
  waiting for transfers between devices: 79.4 us -> 4.3 us
  Pallas kernels: 0 us -> 73.7 us
  local copies, waits for them, and re-layouts: 27.7 us -> 3.64 us
  matrix products: 20 us -> 0 us
  between operations: 16.6 us -> 0.72 us
    all_gather x17 -> x0, blocking collectives: 232 us -> none  [the longest x16 208 us: collected_together(): both, at, found = (lax.all_gather(jnp.concatenate(lines), axis), 0, {})]
    all_to_all x0 -> x6, blocking collectives: none -> 81.3 us  [exchange(): return lax.all_to_all(array, axes, 0, 0, tiled=True)]
    unnamed x2 -> x0, waiting for transfers between devices: 79.4 us -> none
    pallas_call x0 -> x8, Pallas kernels: none -> 73.7 us  [run(): pl.pallas_call(body, out_shape=outs, in_specs=specs, out_specs=jax.tree.m...]
    reduce_sum x9 -> x0, other arithmetic: 61.8 us -> none  [the longest x8 61.1 us: visit(): row_sum = jnp.sum(row_exp, axis=1)]
    reduce_max x8 -> x0, other arithmetic: 47.5 us -> none  [visit(): row_top = jnp.max(jnp.where(alive, toward, lowest), axis=1)]
    dot_general x2 -> x0, matrix products: 20 us -> none  [visit(): pulled = jnp.dot(row_exp, targets.T, precision=lax.Precision.HIGHEST).T]
    psum x1 -> x0, blocking collectives: 18 us -> none  [local(): src_total = lax.psum(jnp.sum(src_weight), 'row')]
  transfers between devices with their start and end apart: 1 -> 1, of which waited for: 1 -> 1; matrix products, arithmetic and copies ran while one was open for 3% -> 0% of each run, Pallas kernels for 0% -> 0%
where the time goes in v1:
time: 169 us; the launch traced here: 168 us
  blocking collectives  81.3 us (48%)
  Pallas kernels  73.7 us (44%)
  starting transfers between devices  4.83 us (3%)
  waiting for transfers between devices  4.3 us (3%)
  local copies, waits for them, and re-layouts  3.64 us (2%)
    all_to_all x6, blocking collectives, exchange(): return lax.all_to_all(array, axes, 0, 0, tiled=True)  81.3 us
    pallas_call x8, Pallas kernels, run(): pl.pallas_call(body, out_shape=outs, in_specs=specs, out_specs=jax.tree.m...  73.7 us
    all_to_all x1, starting transfers between devices, exchange(): return lax.all_to_all(array, axes, 0, 0, tiled=True)  4.83 us
    all_to_all x1, waiting for transfers between devices, exchange(): return lax.all_to_all(array, axes, 0, 0, tiled=True)  4.3 us
  transfers between devices with their start and end apart: 1, of which 1 were waited for; matrix products, arithmetic and copies ran while one was open for 0% of the time, Pallas kernels for 0%

profile of v1, /device:TPU:1, one launch (start us, length us, event | category | flops | bytes accessed | tf_op | source)
XLA Modules:
  0.0 168.5 jit_solution(4410663435439138343)
XLA Ops:
  0.6 0.0 copy-start.3
  0.6 0.8 copy.11.mask_ref
  1.4 0.0 copy-start.5
  1.4 0.0 copy-start.4
  1.4 0.0 copy-done.3
  1.4 0.7 copy-done.5
  2.1 0.0 copy-done.4
  2.1 0.0 copy-start.1
  2.1 0.0 copy-start.2
  2.1 0.7 shard_map.94
  2.8 4.8 %all-to-all-start = ((f32[4,16,128]{2,1,0:T(8,128)}), f32[4,16,128]{2,1,0:T(8,128)S(1)}, u32[]{:S(2)}, u32[]{:S(2)}) async-start(f32[4,16,128]{2,1,0:T(8,128)} %shard_map.94), calls=%async_computation | async-start | bytes 65536 | tf_op jit(solution)/shard_map/all_to_all | solution.py:383
  7.6 4.3 %all-to-all-done.got_ref = f32[4,16,128]{2,1,0:T(8,128)S(1)} async-done(((f32[4,16,128]{2,1,0:T(8,128)}), f32[4,16,128]{2,1,0:T(8,128)S(1)}, u32[]{:S(2)}, u32[]{:S(2)}) %all-to-all-start) | async-done | bytes 32800 | tf_op jit(solution)/shard_map/all_to_all | solution.py:383
  11.9 0.0 copy-done.1
  11.9 0.0 copy-done.2
  11.9 0.0 copy-start
  11.9 0.9 copy-done
  12.9 14.5 %shard_map.95 = (f32[16,4096]{1,0:T(8,128)S(1)}, f32[16,1024]{1,0:T(8,128)S(1)}, f32[8,4224]{1,0:T(8,128)S(1)}) custom-call(s32[1]{0:T(128)} %bitcast.quarter_ref, f32[4,16,128]{2,1,0:T(8,128)S(1)} %all-to-all-done.got_ref, f32[3,16384]{1,0:T(4,128)S(1)} %copy-done, f32[128,128]{1,0:T(8,128)S(1)} %bitcast.31, s32[128,128]{1,0:T(8,128)S(1)} %bitcast.32), custom_call_target="tpu_custom_call" | custom-call | tf_op jit(solution)/shard_map/pallas_call | solution.py:38
  27.3 0.1 copy.12
  27.5 11.6 %all_to_all.59 = f32[8,1,4224]{2,1,0:T(1,128)S(1)} all-to-all(f32[8,1,4224]{2,1,0:T(1,128)S(1)} %copy.12), channel_id=1, replica_groups=mesh['row'=8,'y'=4,'x'=4,'core'=2] {'y','core'}, dimensions={0} | all-to-all | bytes 270336 | tf_op jit(solution)/shard_map/all_to_all | solution.py:383
  39.2 14.3 %shard_map.96 = (f32[2,4096]{1,0:T(2,128)S(1)}, f32[32,2176]{1,0:T(8,128)S(1)}) custom-call(f32[8,4224]{1,0:T(8,128)S(1)} %bitcast.27, f32[16,4096]{1,0:T(8,128)S(1)} %get-tuple-element.15.src_ref, f32[16,1024]{1,0:T(8,128)S(1)} %get-tuple-element.16.tgt_ref), custom_call_target="tpu_custom_call" | custom-call | tf_op jit(solution)/shard_map/pallas_call | solution.py:38
  53.5 0.3 copy.13
  53.8 20.7 %all_to_all.60 = f32[32,1,2176]{2,1,0:T(1,128)S(1)} all-to-all(f32[32,1,2176]{2,1,0:T(1,128)S(1)} %copy.13), channel_id=1, replica_groups=mesh['row'=8,'y'=4,'x'=4,'core'=2] {'row','x'}, dimensions={0} | all-to-all | bytes 557056 | tf_op jit(solution)/shard_map/all_to_all | solution.py:383
  74.5 17.0 %shard_map.97 = (f32[2,1024]{1,0:T(2,128)S(1)}, f32[8,8192]{1,0:T(8,128)S(1)}) custom-call(f32[32,2176]{1,0:T(8,128)S(1)} %bitcast.23, f32[16,4096]{1,0:T(8,128)S(1)} %get-tuple-element.15.src_ref, f32[16,1024]{1,0:T(8,128)S(1)} %get-tuple-element.16.tgt_ref), custom_call_target="tpu_custom_call" | custom-call | tf_op jit(solution)/shard_map/pallas_call | solution.py:38
  91.5 0.3 copy.14
  91.8 11.0 %all_to_all.61 = f32[8,1,8192]{2,1,0:T(1,128)S(1)} all-to-all(f32[8,1,8192]{2,1,0:T(1,128)S(1)} %copy.14), channel_id=1, replica_groups=mesh['row'=8,'y'=4,'x'=4,'core'=2] {'y','core'}, dimensions={0} | all-to-all | bytes 524288 | tf_op jit(solution)/shard_map/all_to_all | solution.py:383
  102.8 0.2 copy.26
  103.0 14.3 %shard_map.98 = f32[32,2048]{1,0:T(8,128)S(1)} custom-call(f32[8,8192]{1,0:T(8,128)S(1)} %bitcast.24, f32[16,4096]{1,0:T(8,128)S(1)} %get-tuple-element.15.src_ref, f32[16,1024]{1,0:T(8,128)S(1)} %get-tuple-element.16.tgt_ref, f32[2,4096]{1,0:T(2,128)S(1)} %get-tuple-element.19.field_ref.scale_ref), custom_call_target="tpu_custom_call" | custom-call | tf_op jit(solution)/shard_map/pallas_call | solution.py:38
  117.3 0.3 copy.15
  117.6 14.3 %all_to_all.62 = f32[32,1,2048]{2,1,0:T(1,128)S(1)} all-to-all(f32[32,1,2048]{2,1,0:T(1,128)S(1)} %copy.15), channel_id=1, replica_groups=mesh['row'=8,'y'=4,'x'=4,'core'=2] {'row','x'}, dimensions={0} | all-to-all | bytes 524288 | tf_op jit(solution)/shard_map/all_to_all | solution.py:383
  131.9 0.1 copy.25
  132.0 12.1 %shard_map.99 = (f32[8,4,512]{2,1,0:T(4,128)S(1)}, f32[1,256]{1,0:T(1,128)}) custom-call(s32[1]{0:T(128)} %bitcast.quarter_ref, f32[32,2048]{1,0:T(8,128)S(1)} %bitcast.26, f32[16,4096]{1,0:T(8,128)S(1)} %get-tuple-element.15.src_ref, f32[16,1024]{1,0:T(8,128)S(1)} %get-tuple-element.16.tgt_ref, f32[2,1024]{1,0:T(2,128)S(1)} %get-tuple-element.20.field_ref, ...), custom_call_target="tpu_custom_call" | custom-call | tf_op jit(solution)/shard_map/pallas_call | solution.py:38
  144.1 10.2 %all_to_all.63.got_ref = f32[8,4,512]{2,1,0:T(4,128)S(1)} all-to-all(f32[8,4,512]{2,1,0:T(4,128)S(1)} %get-tuple-element.21), channel_id=1, replica_groups=mesh['row'=8,'y'=4,'x'=4,'core'=2] {'y','core'}, dimensions={0} | all-to-all | bytes 131072 | tf_op jit(solution)/shard_map/all_to_all | solution.py:383
  154.3 0.1 shard_map.100
  154.4 13.4 %all_to_all.64.got_ref = f32[32,4,512]{2,1,0:T(4,128)S(1)} all-to-all(f32[32,4,512]{2,1,0:T(4,128)S(1)} %shard_map.100), channel_id=1, replica_groups=mesh['row'=8,'y'=4,'x'=4,'core'=2] {'x','y','core'}, dimensions={0} | all-to-all | bytes 524288 | tf_op jit(solution)/shard_map/all_to_all | solution.py:383
  167.7 0.8 shard_map.101
  (2 shorter events, 0.0 us)
Async XLA Ops:
  0.6 0.8 copy-start.3
  1.4 0.7 copy-start.5
  1.4 0.7 copy-start.4
  2.1 9.8 %copy-start.1 = (f32[16384]{0:T(1024)S(1)}, f32[16384]{0:T(1024)}, u32[]{:S(2)}) copy-start(f32[16384]{0:T(1024)} %param.9) | copy-start | bytes 196612
  2.1 9.8 %copy-start.2 = (s32[16384]{0:T(1024)S(1)}, s32[16384]{0:T(1024)}, u32[]{:S(2)}) copy-start(s32[16384]{0:T(1024)} %param.11) | copy-start | bytes 196612
  2.8 9.1 %all-to-all-start = ((f32[4,16,128]{2,1,0:T(8,128)}), f32[4,16,128]{2,1,0:T(8,128)S(1)}, u32[]{:S(2)}, u32[]{:S(2)}) async-start(f32[4,16,128]{2,1,0:T(8,128)} %shard_map.94), calls=%async_computation | async-start | bytes 65536 | tf_op jit(solution)/shard_map/all_to_all | solution.py:383
  11.9 1.0 copy-start

commit v2 on v1

v2 whole, which is shorter than its diff:
```python
import jax
import jax.numpy as jnp
from jax import lax
from jax.experimental import pallas as pl
from jax.experimental.pallas import tpu as pltpu
from jax.sharding import Mesh
from jax.sharding import PartitionSpec as P

epsilon = 0.4
LOG2E = 1.4426950408889634
LN2 = 0.6931471805599453
ALPHA = LOG2E / epsilon
HALF = 0.5 * ALPHA
UNIT = epsilon * LN2
CENTRE = 7.5
LOWEST = -(2.0**100)
TILE = 256
LANES = 128

ROW = "row"
SPLIT = ("x",)
MERGE = ("y", "core")
COLS = ("y", "x", "core")

BIAS_S, BIAS_T, MASK0, LOG_S, RAW_S, LOG_T = 3, 4, 5, 9, 10, 13


def f32(shape):
    return jax.ShapeDtypeStruct(shape, jnp.float32)


def call(body, outs, scratch=(), smem=()):
    def run(*args):
        specs = [
            pl.BlockSpec(memory_space=pltpu.SMEM if k in smem else pltpu.VMEM)
            for k in range(len(args))
        ]
        return pl.pallas_call(
            body,
            out_shape=outs,
            in_specs=specs,
            out_specs=jax.tree.map(lambda _: pl.BlockSpec(memory_space=pltpu.VMEM), outs),
            scratch_shapes=list(scratch),
            compiler_params=pltpu.CompilerParams(vmem_limit_bytes=48 << 20),
        )(*args)

    return run


def parts(u):
    hi = u.astype(jnp.bfloat16)
    rest = u - hi.astype(jnp.float32)
    mid = rest.astype(jnp.bfloat16)
    low = (rest - mid.astype(jnp.float32)).astype(jnp.bfloat16)
    return hi, mid, low


def right_side(u, out_ref):
    hi, mid, low = parts(u)
    zero = jnp.zeros_like(hi)
    out_ref[...] = jnp.concatenate([hi, mid, hi, mid, low, hi, zero, zero], axis=0)


def left_side(u, out_ref):
    hi, mid, low = (p.astype(jnp.float32) for p in parts(u))
    zero = jnp.zeros_like(hi)
    stacked = jnp.concatenate([hi, hi, mid, mid, hi, low, zero, zero], axis=0)
    for c in range(u.shape[1] // LANES):
        block = stacked[:, c * LANES : (c + 1) * LANES]
        out_ref[c * LANES : (c + 1) * LANES, :] = block.T.astype(jnp.bfloat16)


def with_row(u, at, row):
    rows = lax.broadcasted_iota(jnp.int32, u.shape, 0)
    return jnp.where(rows == at, row, u)


def pipelined(steps, fill, drain, buffers):
    one, two = buffers
    fill(0, *one)

    def pair(i, carry):
        fill(2 * i + 1, *two)
        drain(2 * i, *one)
        fill(jnp.minimum(2 * i + 2, steps - 1), *one)
        drain(2 * i + 1, *two)
        return carry

    lax.fori_loop(0, steps // 2, pair, 0)


def row_pass(left_ref, right_ref, buffers, emit, pull_ref=None):
    def fill(b, x_ref, top_ref):
        at = pl.multiple_of(b * TILE, TILE)
        x = jnp.dot(
            left_ref[...], right_ref[:, pl.ds(at, TILE)], preferred_element_type=jnp.float32
        )
        x_ref[...] = x
        top_ref[...] = jnp.max(x.reshape(-1, 8, TILE), axis=0)

    def drain(b, x_ref, top_ref):
        top = top_ref[...]
        p = jnp.exp2(x_ref[...].reshape(-1, 8, TILE) - top[None])
        total = jnp.sum(p, axis=0)
        peak = jnp.max(top, axis=0, keepdims=True)
        weight = jnp.exp2(top - peak)
        sums = jnp.sum(total * weight, axis=0, keepdims=True)
        lines = [peak + jnp.log2(sums)]
        if pull_ref is not None:
            for d in range(3):
                wide = pull_ref[d]
                wide = jnp.concatenate([wide] * (TILE // LANES), axis=1)
                moved = jnp.sum(p * wide.reshape(-1, 8, TILE), axis=0)
                lines.append(jnp.sum(moved * weight, axis=0, keepdims=True) / sums)
        for k in range(TILE // LANES):
            emit(
                b * (TILE // LANES) + k,
                [line[:, k * LANES : (k + 1) * LANES] for line in lines],
            )

    pipelined(right_ref.shape[1] // TILE, fill, drain, buffers)


def col_pass(left_ref, right_ref, buffers, top_ref, sum_ref):
    m = left_ref.shape[0]
    width = buffers[0][0].shape[1]
    cuts = [slice(k * LANES, (k + 1) * LANES) for k in range(width // LANES)]
    blocks = right_ref.shape[1] // width
    top_ref[...] = jnp.full(top_ref.shape, 2.0 * LOWEST, jnp.float32)
    sum_ref[...] = jnp.zeros(sum_ref.shape, jnp.float32)

    def place(s):
        t = s // blocks
        return pl.multiple_of(t * TILE, TILE), pl.multiple_of((s - t * blocks) * width, width)

    def fill(s, x_ref, peak_ref):
        row, at = place(s)
        x = jnp.dot(
            left_ref[pl.ds(row, TILE), :],
            right_ref[:, pl.ds(at, width)],
            preferred_element_type=jnp.float32,
        )
        x_ref[...] = x
        peak = x[:, cuts[0]]
        for cut in cuts[1:]:
            peak = jnp.maximum(peak, x[:, cut])
        peak_ref[...] = peak

    def drain(s, x_ref, peak_ref):
        row, _ = place(s)
        old = top_ref[pl.ds(row, TILE), :]
        top = jnp.maximum(old, peak_ref[...])
        total = sum_ref[pl.ds(row, TILE), :] * jnp.exp2(old - top)
        for cut in cuts:
            total = total + jnp.exp2(x_ref[:, cut] - top)
        top_ref[pl.ds(row, TILE), :] = top
        sum_ref[pl.ds(row, TILE), :] = total

    pipelined((m // TILE) * blocks, fill, drain, buffers)
    found = []
    for c in range(m // LANES):
        top = top_ref[c * LANES : (c + 1) * LANES, :].T
        total = sum_ref[c * LANES : (c + 1) * LANES, :].T
        peak = jnp.max(top, axis=0, keepdims=True)
        sums = jnp.sum(total * jnp.exp2(top - peak), axis=0, keepdims=True)
        found.append(peak + jnp.log2(sums))
    return jnp.concatenate(found, axis=0)


def merged(values):
    peak = jnp.max(values, axis=0)
    return peak + jnp.log2(jnp.sum(jnp.exp2(values - peak[None]), axis=0))


def total_of(pieces):
    return jnp.log2(jnp.sum(pieces, axis=0))


def flat_add(u_ref, row, lines, base=None):
    for c in range(lines.shape[0]):
        lanes = slice(c * LANES, (c + 1) * LANES)
        line = lines[c : c + 1, :]
        if base is not None:
            line = line + base[:, lanes]
        u_ref[row : row + 1, lanes] = line


def mirrored(out_ref, lines):
    for k in range(out_ref.shape[0]):
        out_ref[k] = lines


def run_cols(src_ref, tgt_ref, out_ref, field, work):
    u_ref, left_ref, right_ref, one, two, peak_one, peak_two, top_ref, sum_ref = work
    left_side(tgt_ref[...], left_ref)
    log_mass = src_ref[LOG_S : LOG_S + 1, :]
    bias = src_ref[BIAS_S : BIAS_S + 1, :] + log_mass
    u_ref[...] = src_ref[...]
    if field is None:
        u_ref[BIAS_S : BIAS_S + 1, :] = bias
    else:
        flat_add(u_ref, BIAS_S, field, bias)
    right_side(u_ref[...], right_ref)
    buffers = ((one, peak_one), (two, peak_two))
    return col_pass(left_ref, right_ref, buffers, top_ref, sum_ref)


def run_rows(src_ref, tgt_ref, emit, field, work, pull_ref=None):
    u_ref, left_ref, right_ref, one, two, peak_one, peak_two = work
    base = tgt_ref[BIAS_T : BIAS_T + 1, :] + tgt_ref[LOG_T : LOG_T + 1, :]
    u_ref[...] = tgt_ref[...]
    if field is None:
        u_ref[BIAS_T : BIAS_T + 1, :] = base
    else:
        flat_add(u_ref, BIAS_T, field, base)
    left_side(u_ref[...], left_ref)
    right_side(src_ref[...], right_ref)
    buffers = ((one, peak_one), (two, peak_two))
    row_pass(left_ref, right_ref, buffers, emit, pull_ref)


def to_lines(line_ref):
    def emit(at, found):
        line_ref[pl.ds(at, 1), :] = found[0]

    return emit


def lane_gather(table, lanes):
    return jnp.take_along_axis(table, lanes, axis=1, mode="promise_in_bounds")


def pack_targets(pos_ref, weight_ref, order_ref, mask_ref, out_ref):
    order = jnp.bitwise_and(order_ref[...], TILE - 1)
    high = jnp.right_shift(order, 7)
    low = jnp.bitwise_and(order, LANES - 1)
    high8 = jnp.concatenate([high] * 4, axis=0)
    low8 = jnp.concatenate([low] * 4, axis=0)
    found = jnp.zeros((8, LANES), jnp.float32)
    for r in range(2):
        lanes = slice(r * LANES, (r + 1) * LANES)
        lines = [jnp.broadcast_to(pos_ref[d : d + 1, lanes], (2, LANES)) for d in range(3)]
        lines.append(jnp.broadcast_to(weight_ref[r : r + 1, :], (2, LANES)))
        table = jnp.concatenate(lines, axis=0)
        found = jnp.where(high8 == r, lane_gather(table, low8), found)
    tiles = mask_ref.shape[0]
    at = lax.broadcasted_iota(jnp.int32, (tiles, LANES), 0)
    lane = lax.broadcasted_iota(jnp.int32, (tiles, LANES), 1)
    kept = jnp.broadcast_to(mask_ref[...].astype(jnp.float32), (tiles, LANES))
    line = jnp.sum(jnp.where(at == lane, kept, 0.0), axis=0, keepdims=True)
    both = jnp.concatenate([found, jnp.broadcast_to(line, (8, LANES))], axis=0)
    for k in range(out_ref.shape[0]):
        out_ref[k] = both


def source_features(quarter_ref, pos_ref, weight_ref, order_ref, src_ref):
    quarter = quarter_ref[0]
    n = src_ref.shape[1]
    lines = n // LANES
    groups = lines // 8
    order = order_ref[pl.ds(pl.multiple_of(quarter * lines, 8), lines), :]
    order = jnp.bitwise_and(order, LANES * LANES - 1)
    high = jnp.right_shift(order, 7)
    low = jnp.bitwise_and(order, LANES - 1)
    highs = [high[8 * g : 8 * g + 8] for g in range(groups)]
    lows = [low[8 * g : 8 * g + 8] for g in range(groups)]

    def look(r, found):
        at = pl.multiple_of(r * LANES, LANES)
        tables = [
            jnp.broadcast_to(pos_ref[d : d + 1, pl.ds(at, LANES)], (8, LANES)) for d in range(3)
        ]
        tables.append(jnp.broadcast_to(weight_ref[pl.ds(r, 1), :], (8, LANES)))
        out = []
        for g in range(groups):
            here = highs[g] == r
            for a in range(4):
                old = found[4 * g + a]
                out.append(jnp.where(here, lane_gather(tables[a], lows[g]), old))
        return tuple(out)

    zero = jnp.zeros((8, LANES), jnp.float32)
    found = lax.fori_loop(0, LANES, look, (zero,) * (4 * groups), unroll=4)

    src_ref[...] = jnp.zeros_like(src_ref)
    for g in range(groups):
        square = jnp.zeros((8, LANES), jnp.float32)
        raw = []
        for d in range(3):
            raw.append(found[4 * g + d] - CENTRE)
            square = square + raw[d] * raw[d]
        rows = {LOG_S: jnp.log2(found[4 * g + 3]), BIAS_S: -HALF * square}
        for d in range(3):
            rows[RAW_S + d] = raw[d]
            rows[d] = ALPHA * raw[d]
        for row, values in rows.items():
            for k in range(8):
                lanes = slice((8 * g + k) * LANES, (8 * g + k + 1) * LANES)
                src_ref[row : row + 1, lanes] = values[k : k + 1, :]
    src_ref[BIAS_T : BIAS_T + 1, :] = jnp.ones((1, n), jnp.float32)


def opening_cols(quarter_ref, got_ref, part_ref, src_ref, tgt_ref, out_ref, *work):
    n = src_ref.shape[1]
    m = tgt_ref.shape[1]
    tiles = got_ref.shape[0]
    flags = jnp.concatenate([got_ref[t][8:9, :] for t in range(tiles)] * 2, axis=0)
    src_tiles = n // TILE
    flags = pltpu.roll(flags, (LANES - quarter_ref[0] * src_tiles) % LANES, 1)
    bias = jnp.where(flags > 0.5, 0.0, LOWEST)
    src_ref[...] = part_ref[...]
    for i in range(src_tiles):
        src_ref[MASK0 : MASK0 + tiles, i * TILE : (i + 1) * TILE] = jnp.broadcast_to(
            bias[:tiles, i : i + 1], (tiles, TILE)
        )
    tgt_ref[...] = jnp.zeros_like(tgt_ref)
    for t in range(tiles):
        for k in range(2):
            lanes = slice(t * TILE + k * LANES, t * TILE + (k + 1) * LANES)
            square = jnp.zeros((1, LANES), jnp.float32)
            for d in range(3):
                raw = got_ref[t][2 * d + k : 2 * d + k + 1, :] - CENTRE
                tgt_ref[d : d + 1, lanes] = raw
                square = square + raw * raw
            tgt_ref[BIAS_T : BIAS_T + 1, lanes] = -HALF * square
            tgt_ref[LOG_T : LOG_T + 1, lanes] = jnp.log2(got_ref[t][6 + k : 7 + k, :])
        tgt_ref[MASK0 + t : MASK0 + t + 1, t * TILE : (t + 1) * TILE] = jnp.ones(
            (1, TILE), jnp.float32
        )
    tgt_ref[BIAS_S : BIAS_S + 1, :] = jnp.ones((1, m), jnp.float32)
    value = run_cols(src_ref, tgt_ref, out_ref, None, work)
    mass = jnp.sum(jnp.exp2(src_ref[LOG_S : LOG_S + 1, :]), axis=1, keepdims=True)
    mirrored(out_ref, jnp.concatenate([value, jnp.broadcast_to(mass, (8, LANES))], axis=0))


def opening_rows(src_ref, tgt_ref, out_ref, line_ref, *work):
    n = src_ref.shape[1]
    run_rows(src_ref, tgt_ref, to_lines(line_ref), None, work)
    mass = jnp.sum(jnp.exp2(tgt_ref[LOG_T : LOG_T + 1, :]), axis=1, keepdims=True)
    line_ref[n // LANES :, :] = jnp.broadcast_to(mass, (8, LANES))
    mirrored(out_ref, line_ref[...])


def second_cols(got_ref, src_ref, tgt_ref, field_ref, out_ref, *work):
    lines = src_ref.shape[1] // LANES
    total = total_of(got_ref[:, lines:, :])
    field = -(merged(got_ref[:, :lines, :]) - total[:1, :1])
    field_ref[:lines, :] = field
    field_ref[lines:, :] = total
    mirrored(out_ref, run_cols(src_ref, tgt_ref, out_ref, field, work))


def second_rows(got_ref, src_ref, tgt_ref, field_ref, out_ref, line_ref, *work):
    lines = tgt_ref.shape[1] // LANES
    total = total_of(got_ref[:, lines:, :])
    field = -(merged(got_ref[:, :lines, :]) - total[:1, :1])
    field_ref[:lines, :] = field
    field_ref[lines:, :] = total
    run_rows(src_ref, tgt_ref, to_lines(line_ref), field, work)
    mirrored(out_ref, line_ref[...])


def updated(got_ref, field_ref):
    lines = field_ref.shape[0] - 8
    total = field_ref[lines:, :]
    return 0.5 * (field_ref[:lines, :] - (merged(got_ref[...]) - total[:1, :1])), total


def sweep_cols(got_ref, old_ref, src_ref, tgt_ref, field_ref, out_ref, *work):
    field, total = updated(got_ref, old_ref)
    field_ref[: field.shape[0], :] = field
    field_ref[field.shape[0] :, :] = total
    mirrored(out_ref, run_cols(src_ref, tgt_ref, out_ref, field, work))


def sweep_rows(got_ref, old_ref, src_ref, tgt_ref, field_ref, out_ref, line_ref, *work):
    field, total = updated(got_ref, old_ref)
    field_ref[: field.shape[0], :] = field
    field_ref[field.shape[0] :, :] = total
    run_rows(src_ref, tgt_ref, to_lines(line_ref), field, work)
    mirrored(out_ref, line_ref[...])


def last_rows(got_ref, old_ref, scale_ref, src_ref, tgt_ref, out_ref, pull_ref, *work):
    field, _ = updated(got_ref, old_ref)
    for d in range(3):
        for c in range(tgt_ref.shape[1] // LANES):
            lanes = slice(c * LANES, (c + 1) * LANES)
            wide = jnp.broadcast_to(tgt_ref[d : d + 1, lanes], (LANES, LANES))
            pull_ref[d, lanes, :] = wide.T
    lines = src_ref.shape[1] // LANES
    total = scale_ref[lines : lines + 1, 0:1]
    share = lines // out_ref.shape[0]

    def emit(at, found):
        piece = at // share
        row = at - piece * share
        out_ref[piece, pl.ds(row, 1), :] = found[0] - total
        lanes = pl.ds(pl.multiple_of(at * LANES, LANES), LANES)
        for d in range(3):
            raw = src_ref[RAW_S + d : RAW_S + d + 1, lanes]
            out_ref[piece, pl.ds(row + (d + 1) * share, 1), :] = raw - found[d + 1]

    run_rows(src_ref, tgt_ref, emit, field, work, pull_ref)


def closing(got_ref, out_ref):
    share = got_ref.shape[1] // 4
    values = got_ref[:, :share, :]
    peak = jnp.max(values, axis=0)
    weight = jnp.exp2(values - peak[None])
    total = jnp.sum(weight, axis=0)
    lines = [-UNIT * (peak + jnp.log2(total))]
    for d in range(3):
        piece = got_ref[:, (d + 1) * share : (d + 2) * share, :]
        lines.append(jnp.sum(weight * piece, axis=0) / total)
    mirrored(out_ref, jnp.concatenate(lines, axis=0))


def spread(quarter_ref, got_ref, col_ref, scale_ref, value_ref, shift_ref, own_ref, line_ref):
    share = got_ref.shape[1] // 4
    for k in range(got_ref.shape[0]):
        for r in range(share):
            lanes = slice((k * share + r) * LANES, (k * share + r + 1) * LANES)
            value_ref[:, lanes] = got_ref[k][r : r + 1, :]
            for d in range(3):
                row = (d + 1) * share + r
                shift_ref[d : d + 1, lanes] = got_ref[k][row : row + 1, :]
    lines = col_ref.shape[1]
    total = scale_ref[lines : lines + 1, 0:1]
    line_ref[...] = -UNIT * (merged(col_ref[...]) - total)
    for k in range(2):
        row = 2 * quarter_ref[0] + k
        own_ref[:, k * LANES : (k + 1) * LANES] = line_ref[pl.ds(row, 1), :]


def exchange(array, axes):
    return lax.all_to_all(array, axes, 0, 0, tiled=True)


def local(src_pos, tgt_pos, src_weight, tgt_weight, src_order, tgt_order, tile_mask):
    rows_here = src_pos.shape[1]
    splits = lax.axis_size(SPLIT)
    merges = lax.axis_size(MERGE)
    heights = lax.axis_size((ROW,) + SPLIT)
    everyone = SPLIT + MERGE
    n = rows_here // splits
    m = tgt_pos.shape[1] * splits
    nl, ml = n // LANES, m // LANES
    quarter = lax.axis_index(SPLIT).astype(jnp.int32).reshape(1)
    left = pltpu.VMEM((m, LANES), jnp.bfloat16)
    right = pltpu.VMEM((LANES, n), jnp.bfloat16)

    def vm(*shape):
        return pltpu.VMEM(shape, jnp.float32)

    wide = 1024
    col_work = (vm(16, n), left, right, vm(TILE, wide), vm(TILE, wide))
    col_work += (vm(TILE, LANES), vm(TILE, LANES), vm(m, LANES), vm(m, LANES))
    row_work = (vm(16, m), left, right, vm(m, TILE), vm(m, TILE), vm(8, TILE), vm(8, TILE))
    src_shape, tgt_shape = f32((16, n)), f32((16, m))
    field_s, field_t = f32((nl + 8, LANES)), f32((ml + 8, LANES))
    to_cols, to_rows = f32((heights, ml, LANES)), f32((merges, nl, LANES))
    heads = (ROW,) + SPLIT

    packed = call(pack_targets, f32((splits, 16, LANES)))(
        tgt_pos, tgt_weight.reshape(-1, LANES), tgt_order.reshape(-1, LANES), tile_mask
    )
    packed = exchange(packed, SPLIT)
    part = call(source_features, src_shape, (), (0,))(
        quarter, src_pos, src_weight.reshape(-1, LANES), src_order.reshape(-1, LANES)
    )
    src, tgt, col0 = call(
        opening_cols, (src_shape, tgt_shape, f32((heights, ml + 8, LANES))), col_work, (0,)
    )(quarter, packed, part)
    col0 = exchange(col0, heads)
    row0 = call(opening_rows, f32((merges, nl + 8, LANES)), (vm(nl + 8, LANES),) + row_work)(
        src, tgt
    )
    row0 = exchange(row0, MERGE)
    f0, col1 = call(second_cols, (field_s, to_cols), col_work)(row0, src, tgt)
    col1 = exchange(col1, heads)
    line = (vm(nl, LANES),)
    g0, row1 = call(second_rows, (field_t, to_rows), line + row_work)(col0, src, tgt)
    row1 = exchange(row1, MERGE)
    g1, row2 = call(sweep_rows, (field_t, to_rows), line + row_work)(col1, g0, src, tgt)
    row2 = exchange(row2, MERGE)
    f1, col2 = call(sweep_cols, (field_s, to_cols), col_work)(row1, f0, src, tgt)
    col2 = exchange(col2, heads)
    _, col3 = call(sweep_cols, (field_s, to_cols), col_work)(row2, f1, src, tgt)
    col3 = exchange(col3, heads)
    row3 = call(last_rows, f32((merges, 4 * (nl // merges), LANES)), (vm(3, m, LANES),) + row_work)(
        col2, g1, f1, src, tgt
    )
    row3 = exchange(row3, MERGE)
    done = call(closing, f32((lax.axis_size(everyone), 4 * (nl // merges), LANES)))(row3)
    done = exchange(done, everyone)
    value, shift, own = call(
        spread, (f32((1, rows_here)), f32((3, rows_here)), f32((1, TILE))), (vm(ml, LANES),), (0,)
    )(quarter, done, col3, g1)
    return value.reshape(-1), own.reshape(-1), shift


def solution(mesh):
    split = Mesh(mesh.devices.reshape(mesh.shape["row"], 4, 4, 2), ("row", "y", "x", "core"))
    in_specs = (P(None, ROW), P(None, COLS), P(ROW), P(COLS), P(ROW), P(COLS), P(ROW, COLS))
    out_specs = (P(ROW), P(COLS), P(None, ROW))
    return jax.shard_map(local, mesh=split, in_specs=in_specs, out_specs=out_specs, check_vma=False)
```

time: 169 us -> 159 us (0.941)
  blocking collectives: 81.3 us -> 15.5 us
  starting transfers between devices: 4.83 us -> 55.4 us
  waiting for transfers between devices: 4.3 us -> 20.1 us
  Pallas kernels: 73.7 us -> 64.1 us
    all_to_all x6 -> x1, blocking collectives: 81.3 us -> 15.5 us  [exchange(): return lax.all_to_all(array, axes, 0, 0, tiled=True)]
    all_to_all x1 -> x9, starting transfers between devices: 4.83 us -> 55.4 us  [exchange(): return lax.all_to_all(array, axes, 0, 0, tiled=True)]
    all_to_all x1 -> x9, waiting for transfers between devices: 4.3 us -> 20.1 us  [exchange(): return lax.all_to_all(array, axes, 0, 0, tiled=True)]
    pallas_call x8 -> x12, Pallas kernels: 73.7 us -> 64.1 us  [run(): pl.pallas_call(body, out_shape=outs, in_specs=specs, out_specs=jax.tree.m...]
  transfers between devices with their start and end apart: 1 -> 9, of which waited for: 1 -> 4; matrix products, arithmetic and copies ran while one was open for 0% -> 0% of each run, Pallas kernels for 0% -> 35%
where the time goes in v2:
time: 159 us; the launch traced here: 158 us
  Pallas kernels  64.1 us (40%)
  starting transfers between devices  55.4 us (35%)
  waiting for transfers between devices  20.1 us (13%)
  blocking collectives  15.5 us (10%)
  local copies, waits for them, and re-layouts  2.38 us (1%)
    pallas_call x12, Pallas kernels, run(): pl.pallas_call(body, out_shape=outs, in_specs=specs, out_specs=jax.tree.m...  64.1 us
    all_to_all x9, starting transfers between devices, exchange(): return lax.all_to_all(array, axes, 0, 0, tiled=True)  55.4 us
    all_to_all x9, waiting for transfers between devices, exchange(): return lax.all_to_all(array, axes, 0, 0, tiled=True)  20.1 us
    all_to_all x1, blocking collectives, exchange(): return lax.all_to_all(array, axes, 0, 0, tiled=True)  15.5 us
  transfers between devices with their start and end apart: 9, of which 4 were waited for; matrix products, arithmetic and copies ran while one was open for 0% of the time, Pallas kernels for 35%

profile of v2, /device:TPU:1, one launch (start us, length us, event | category | flops | bytes accessed | tf_op | source)
XLA Modules:
  0.0 158.2 jit_solution(12712707882168657664)
XLA Ops:
  0.6 0.0 copy-start.3
  0.6 0.8 copy.10.mask_ref
  1.4 0.0 copy-start.5
  1.4 0.0 copy-start.4
  1.4 0.0 copy-done.3
  1.4 0.7 copy-done.5
  2.1 0.0 copy-done.4
  2.1 0.0 copy-start.1
  2.1 0.0 copy-start.2
  2.1 0.7 shard_map.94
  2.8 4.8 %all-to-all-start = ((f32[4,16,128]{2,1,0:T(8,128)}), f32[4,16,128]{2,1,0:T(8,128)S(1)}, u32[]{:S(2)}, u32[]{:S(2)}) async-start(f32[4,16,128]{2,1,0:T(8,128)} %shard_map.94), calls=%async_computation | async-start | bytes 65536 | tf_op jit(solution)/shard_map/all_to_all | solution.py:438
  7.6 0.0 copy-done.1
  7.6 0.0 copy-done.2
  7.6 0.0 copy-start
  7.6 0.9 copy-done
  8.6 6.0 %shard_map.95.part_ref = f32[16,4096]{1,0:T(8,128)S(1)} custom-call(s32[1]{0:T(128)} %bitcast.quarter_ref, f32[3,16384]{1,0:T(4,128)S(1)} %copy-done, f32[128,128]{1,0:T(8,128)S(1)} %bitcast.7, s32[128,128]{1,0:T(8,128)S(1)} %bitcast.8), custom_call_target="tpu_custom_call" | custom-call | tf_op jit(solution)/shard_map/pallas_call | solution.py:38
  14.5 0.0 all-to-all-done.got_ref
  14.6 6.8 %shard_map.96 = (f32[16,4096]{1,0:T(8,128)S(1)}, f32[16,1024]{1,0:T(8,128)S(1)}, f32[32,16,128]{2,1,0:T(8,128)}) custom-call(s32[1]{0:T(128)} %bitcast.quarter_ref, f32[4,16,128]{2,1,0:T(8,128)S(1)} %all-to-all-done.got_ref, f32[16,4096]{1,0:T(8,128)S(1)} %shard_map.95.part_ref), custom_call_target="tpu_custom_call" | custom-call | tf_op jit(solution)/shard_map/pallas_call | solution.py:38
  21.4 11.3 %all-to-all-start.1 = ((f32[32,16,128]{2,1,0:T(8,128)}), f32[32,16,128]{2,1,0:T(8,128)S(1)}, u32[]{:S(2)}, u32[]{:S(2)}) async-start(f32[32,16,128]{2,1,0:T(8,128)} %get-tuple-element.18), calls=%async_computation.1 | async-start | bytes 524288 | tf_op jit(solution)/shard_map/all_to_all | solution.py:438
  32.6 6.5 %shard_map.98 = f32[8,40,128]{2,1,0:T(8,128)} custom-call(f32[16,4096]{1,0:T(8,128)S(1)} %get-tuple-element.19.src_ref, f32[16,1024]{1,0:T(8,128)S(1)} %get-tuple-element.20.tgt_ref), custom_call_target="tpu_custom_call" | custom-call | tf_op jit(solution)/shard_map/pallas_call | solution.py:38
  39.1 4.2 %all-to-all-done.1.got_ref = f32[32,16,128]{2,1,0:T(8,128)S(1)} async-done(((f32[32,16,128]{2,1,0:T(8,128)}), f32[32,16,128]{2,1,0:T(8,128)S(1)}, u32[]{:S(2)}, u32[]{:S(2)}) %all-to-all-start.1) | async-done | bytes 262176 | tf_op jit(solution)/shard_map/all_to_all | solution.py:438
  43.3 7.7 %all-to-all-start.3 = ((f32[8,40,128]{2,1,0:T(8,128)}), f32[8,40,128]{2,1,0:T(8,128)S(1)}, u32[]{:S(2)}, u32[]{:S(2)}) async-start(f32[8,40,128]{2,1,0:T(8,128)} %shard_map.98), calls=%async_computation.3 | async-start | bytes 327680 | tf_op jit(solution)/shard_map/all_to_all | solution.py:438
  51.0 6.4 %shard_map.97 = (f32[16,128]{1,0:T(8,128)S(1)}, f32[8,32,128]{2,1,0:T(8,128)}) custom-call(f32[32,16,128]{2,1,0:T(8,128)S(1)} %all-to-all-done.1.got_ref, f32[16,4096]{1,0:T(8,128)S(1)} %get-tuple-element.19.src_ref, f32[16,1024]{1,0:T(8,128)S(1)} %get-tuple-element.20.tgt_ref), custom_call_target="tpu_custom_call" | custom-call | tf_op jit(solution)/shard_map/pallas_call | solution.py:38
  57.4 0.0 all-to-all-done.3.got_ref
  57.4 4.8 %all-to-all-start.2 = ((f32[8,32,128]{2,1,0:T(8,128)}), f32[8,32,128]{2,1,0:T(8,128)S(1)}, u32[]{:S(2)}, u32[]{:S(2)}) async-start(f32[8,32,128]{2,1,0:T(8,128)} %get-tuple-element.21), calls=%async_computation.2 | async-start | bytes 262144 | tf_op jit(solution)/shard_map/all_to_all | solution.py:438
  62.2 6.8 %shard_map.99 = (f32[40,128]{1,0:T(8,128)S(1)}, f32[32,8,128]{2,1,0:T(8,128)}) custom-call(f32[8,40,128]{2,1,0:T(8,128)S(1)} %all-to-all-done.3.got_ref, f32[16,4096]{1,0:T(8,128)S(1)} %get-tuple-element.19.src_ref, f32[16,1024]{1,0:T(8,128)S(1)} %get-tuple-element.20.tgt_ref), custom_call_target="tpu_custom_call" | custom-call | tf_op jit(solution)/shard_map/pallas_call | solution.py:38
  69.0 0.0 all-to-all-done.2.got_ref
  69.0 3.8 %all-to-all-start.5 = ((f32[32,8,128]{2,1,0:T(8,128)}), f32[32,8,128]{2,1,0:T(8,128)S(1)}, u32[]{:S(2)}, u32[]{:S(2)}) async-start(f32[32,8,128]{2,1,0:T(8,128)} %get-tuple-element.24), calls=%async_computation.5 | async-start | bytes 262144 | tf_op jit(solution)/shard_map/all_to_all | solution.py:438
  72.8 6.8 %shard_map.100 = (f32[40,128]{1,0:T(8,128)S(1)}, f32[32,8,128]{2,1,0:T(8,128)}) custom-call(f32[8,32,128]{2,1,0:T(8,128)S(1)} %all-to-all-done.2.got_ref, f32[40,128]{1,0:T(8,128)S(1)} %get-tuple-element.22.old_ref, f32[16,4096]{1,0:T(8,128)S(1)} %get-tuple-element.19.src_ref, f32[16,1024]{1,0:T(8,128)S(1)} %get-tuple-element.20.tgt_ref), custom_call_target="tpu_custom_call" | custom-call | tf_op jit(solution)/shard_map/pallas_call | solution.py:38
  79.6 3.1 %all-to-all-done.5.got_ref = f32[32,8,128]{2,1,0:T(8,128)S(1)} async-done(((f32[32,8,128]{2,1,0:T(8,128)}), f32[32,8,128]{2,1,0:T(8,128)S(1)}, u32[]{:S(2)}, u32[]{:S(2)}) %all-to-all-start.5) | async-done | bytes 131104 | tf_op jit(solution)/shard_map/all_to_all | solution.py:438
  82.7 6.1 %all-to-all-start.4 = ((f32[32,8,128]{2,1,0:T(8,128)}), f32[32,8,128]{2,1,0:T(8,128)S(1)}, u32[]{:S(2)}, u32[]{:S(2)}) async-start(f32[32,8,128]{2,1,0:T(8,128)} %get-tuple-element.23), calls=%async_computation.4 | async-start | bytes 262144 | tf_op jit(solution)/shard_map/all_to_all | solution.py:438
  88.8 6.4 %shard_map.101 = (f32[16,128]{1,0:T(8,128)S(1)}, f32[8,32,128]{2,1,0:T(8,128)}) custom-call(f32[32,8,128]{2,1,0:T(8,128)S(1)} %all-to-all-done.5.got_ref, f32[16,128]{1,0:T(8,128)S(1)} %get-tuple-element.25.old_ref, f32[16,4096]{1,0:T(8,128)S(1)} %get-tuple-element.19.src_ref, f32[16,1024]{1,0:T(8,128)S(1)} %get-tuple-element.20.tgt_ref), custom_call_target="tpu_custom_call" | custom-call | tf_op jit(solution)/shard_map/pallas_call | solution.py:38
  95.3 2.9 %all-to-all-done.4.got_ref = f32[32,8,128]{2,1,0:T(8,128)S(1)} async-done(((f32[32,8,128]{2,1,0:T(8,128)}), f32[32,8,128]{2,1,0:T(8,128)S(1)}, u32[]{:S(2)}, u32[]{:S(2)}) %all-to-all-start.4) | async-done | bytes 131104 | tf_op jit(solution)/shard_map/all_to_all | solution.py:438
  98.2 6.6 %all-to-all-start.8 = ((f32[8,32,128]{2,1,0:T(8,128)}), f32[8,32,128]{2,1,0:T(8,128)S(1)}, u32[]{:S(2)}, u32[]{:S(2)}) async-start(f32[8,32,128]{2,1,0:T(8,128)} %get-tuple-element.28), calls=%async_computation.8 | async-start | bytes 262144 | tf_op jit(solution)/shard_map/all_to_all | solution.py:438
  104.8 10.1 %shard_map.102 = f32[8,16,128]{2,1,0:T(8,128)} custom-call(f32[32,8,128]{2,1,0:T(8,128)S(1)} %all-to-all-done.4.got_ref, f32[16,128]{1,0:T(8,128)S(1)} %get-tuple-element.26.old_ref.scale_ref, f32[40,128]{1,0:T(8,128)S(1)} %get-tuple-element.27.scale_ref.old_ref, f32[16,4096]{1,0:T(8,128)S(1)} %get-tuple-element.19.src_ref, ...), custom_call_target="tpu_custom_call" | custom-call | tf_op jit(solution)/shard_map/pallas_call | solution.py:38
  114.8 0.0 all-to-all-done.8.got_ref
  114.8 4.8 %all-to-all-start.6 = ((f32[8,16,128]{2,1,0:T(8,128)}), f32[8,16,128]{2,1,0:T(8,128)S(1)}, u32[]{:S(2)}, u32[]{:S(2)}) async-start(f32[8,16,128]{2,1,0:T(8,128)} %shard_map.102), calls=%async_computation.6 | async-start | bytes 131072 | tf_op jit(solution)/shard_map/all_to_all | solution.py:438
  119.6 6.8 %shard_map.104 = (f32[40,128]{1,0:T(8,128)}, f32[32,8,128]{2,1,0:T(8,128)}) custom-call(f32[8,32,128]{2,1,0:T(8,128)S(1)} %all-to-all-done.8.got_ref, f32[40,128]{1,0:T(8,128)S(1)} %get-tuple-element.27.scale_ref.old_ref, f32[16,4096]{1,0:T(8,128)S(1)} %get-tuple-element.19.src_ref, f32[16,1024]{1,0:T(8,128)S(1)} %get-tuple-element.20.tgt_ref), custom_call_target="tpu_custom_call" | custom-call | tf_op jit(solution)/shard_map/pallas_call | solution.py:38
  126.4 0.0 all-to-all-done.6.got_ref
  126.4 5.4 %all-to-all-start.9 = ((f32[32,8,128]{2,1,0:T(8,128)}), f32[32,8,128]{2,1,0:T(8,128)S(1)}, u32[]{:S(2)}, u32[]{:S(2)}) async-start(f32[32,8,128]{2,1,0:T(8,128)} %get-tuple-element.29), calls=%async_computation.9 | async-start | bytes 262144 | tf_op jit(solution)/shard_map/all_to_all | solution.py:438
  131.9 9.9 %all-to-all-done.9.col_ref = f32[32,8,128]{2,1,0:T(8,128)S(1)} async-done(((f32[32,8,128]{2,1,0:T(8,128)}), f32[32,8,128]{2,1,0:T(8,128)S(1)}, u32[]{:S(2)}, u32[]{:S(2)}) %all-to-all-start.9) | async-done | bytes 131104 | tf_op jit(solution)/shard_map/all_to_all | solution.py:438
  141.8 15.5 %all_to_all.50.got_ref = f32[32,16,128]{2,1,0:T(8,128)S(1)} all-to-all(f32[32,16,128]{2,1,0:T(8,128)S(1)} %shard_map.103), channel_id=1, replica_groups=mesh['row'=8,'y'=4,'x'=4,'core'=2] {'x','y','core'}, dimensions={0} | all-to-all | bytes 524288 | tf_op jit(solution)/shard_map/all_to_all | solution.py:438
  157.3 0.9 shard_map.105
  (1 shorter events, 0.0 us)
Async XLA Ops:
  0.6 0.8 copy-start.3
  1.4 0.7 copy-start.5
  1.4 0.7 copy-start.4
  2.1 5.5 %copy-start.1 = (f32[16384]{0:T(1024)S(1)}, f32[16384]{0:T(1024)}, u32[]{:S(2)}) copy-start(f32[16384]{0:T(1024)} %param.9) | copy-start | bytes 196612
  2.1 5.5 %copy-start.2 = (s32[16384]{0:T(1024)S(1)}, s32[16384]{0:T(1024)}, u32[]{:S(2)}) copy-start(s32[16384]{0:T(1024)} %param.11) | copy-start | bytes 196612
  2.8 11.8 %all-to-all-start = ((f32[4,16,128]{2,1,0:T(8,128)}), f32[4,16,128]{2,1,0:T(8,128)S(1)}, u32[]{:S(2)}, u32[]{:S(2)}) async-start(f32[4,16,128]{2,1,0:T(8,128)} %shard_map.94), calls=%async_computation | async-start | bytes 65536 | tf_op jit(solution)/shard_map/all_to_all | solution.py:438
  7.6 1.0 copy-start
  21.4 21.9 %all-to-all-start.1 = ((f32[32,16,128]{2,1,0:T(8,128)}), f32[32,16,128]{2,1,0:T(8,128)S(1)}, u32[]{:S(2)}, u32[]{:S(2)}) async-start(f32[32,16,128]{2,1,0:T(8,128)} %get-tuple-element.18), calls=%async_computation.1 | async-start | bytes 524288 | tf_op jit(solution)/shard_map/all_to_all | solution.py:438
  43.3 14.1 %all-to-all-start.3 = ((f32[8,40,128]{2,1,0:T(8,128)}), f32[8,40,128]{2,1,0:T(8,128)S(1)}, u32[]{:S(2)}, u32[]{:S(2)}) async-start(f32[8,40,128]{2,1,0:T(8,128)} %shard_map.98), calls=%async_computation.3 | async-start | bytes 327680 | tf_op jit(solution)/shard_map/all_to_all | solution.py:438
  57.4 11.6 %all-to-all-start.2 = ((f32[8,32,128]{2,1,0:T(8,128)}), f32[8,32,128]{2,1,0:T(8,128)S(1)}, u32[]{:S(2)}, u32[]{:S(2)}) async-start(f32[8,32,128]{2,1,0:T(8,128)} %get-tuple-element.21), calls=%async_computation.2 | async-start | bytes 262144 | tf_op jit(solution)/shard_map/all_to_all | solution.py:438
  69.0 13.7 %all-to-all-start.5 = ((f32[32,8,128]{2,1,0:T(8,128)}), f32[32,8,128]{2,1,0:T(8,128)S(1)}, u32[]{:S(2)}, u32[]{:S(2)}) async-start(f32[32,8,128]{2,1,0:T(8,128)} %get-tuple-element.24), calls=%async_computation.5 | async-start | bytes 262144 | tf_op jit(solution)/shard_map/all_to_all | solution.py:438
  82.7 15.5 %all-to-all-start.4 = ((f32[32,8,128]{2,1,0:T(8,128)}), f32[32,8,128]{2,1,0:T(8,128)S(1)}, u32[]{:S(2)}, u32[]{:S(2)}) async-start(f32[32,8,128]{2,1,0:T(8,128)} %get-tuple-element.23), calls=%async_computation.4 | async-start | bytes 262144 | tf_op jit(solution)/shard_map/all_to_all | solution.py:438
  98.2 16.6 %all-to-all-start.8 = ((f32[8,32,128]{2,1,0:T(8,128)}), f32[8,32,128]{2,1,0:T(8,128)S(1)}, u32[]{:S(2)}, u32[]{:S(2)}) async-start(f32[8,32,128]{2,1,0:T(8,128)} %get-tuple-element.28), calls=%async_computation.8 | async-start | bytes 262144 | tf_op jit(solution)/shard_map/all_to_all | solution.py:438
  114.8 11.6 %all-to-all-start.6 = ((f32[8,16,128]{2,1,0:T(8,128)}), f32[8,16,128]{2,1,0:T(8,128)S(1)}, u32[]{:S(2)}, u32[]{:S(2)}) async-start(f32[8,16,128]{2,1,0:T(8,128)} %shard_map.102), calls=%async_computation.6 | async-start | bytes 131072 | tf_op jit(solution)/shard_map/all_to_all | solution.py:438
  126.4 15.4 %all-to-all-start.9 = ((f32[32,8,128]{2,1,0:T(8,128)}), f32[32,8,128]{2,1,0:T(8,128)S(1)}, u32[]{:S(2)}, u32[]{:S(2)}) async-start(f32[32,8,128]{2,1,0:T(8,128)} %get-tuple-element.29), calls=%async_computation.9 | async-start | bytes 262144 | tf_op jit(solution)/shard_map/all_to_all | solution.py:438
